TPU v7x, 32 devices: a whole 2x2x4 slice. The times are simulated.
32 devices in a mesh: rep: 8 (over z, x), fsdp: 4 (over y, core).
Axes of the slice: x: 2, y: 2, z: 4, core: 2. Of those that a mesh axis runs over, the one named last changes fastest.
Arguments:
- images: bfloat16 [512, 197, 384], P(('rep', 'fsdp')), may hold values from -6 to 6
- cotangent: bfloat16 [512, 197, 384], P(('rep', 'fsdp')), may hold values from -6 to 6
- counts: int32 [32], P(('rep', 'fsdp')), may hold values from 1 to 16, as said below
- w_qkv: float32 [384, 1152], P('fsdp'), may hold values from -0.3125 to 0.3125
- w_proj: float32 [384, 384], P('fsdp'), may hold values from -2.5 to 2.5
- w_fc1: float32 [384, 1536], P('fsdp'), may hold values from -0.3125 to 0.3125
- w_fc2: float32 [1536, 384], P(None, 'fsdp'), may hold values from -0.15625 to 0.15625
- gains: float32 [2, 384], P(None, 'fsdp'), may hold values from 0.1 to 1.9
- biases: float32 [10, 384], P(None, 'fsdp'), may hold values from -3 to 3
- mom_qkv: float32 [384, 1152], P('fsdp'), may hold values from -10 to 10
- mom_proj: float32 [384, 384], P('fsdp'), may hold values from -1.75 to 1.75
- mom_fc1: float32 [384, 1536], P('fsdp'), may hold values from -5 to 5
- mom_fc2: float32 [1536, 384], P(None, 'fsdp'), may hold values from -8 to 8
- gains_first: float32 [2, 384], P(None, 'fsdp'), may hold values from -6 to 6
- gains_second: float32 [2, 384], P(None, 'fsdp'), may hold values from 0.985 to 9.85
- biases_first: float32 [10, 384], P(None, 'fsdp'), may hold values from -6 to 6
- biases_second: float32 [10, 384], P(None, 'fsdp'), may hold values from 0.985 to 9.85
Outputs:
- block_output: bfloat16 [512, 197, 384], P(('rep', 'fsdp'))
- input_grad: bfloat16 [512, 197, 384], P(('rep', 'fsdp'))
- grad_qkv: float32 [384, 1152], P('fsdp')
- grad_proj: float32 [384, 384], P('fsdp')
- grad_fc1: float32 [384, 1536], P('fsdp')
- grad_fc2: float32 [1536, 384], P(None, 'fsdp')
- grad_gains: float32 [2, 384], P(None, 'fsdp')
- grad_biases: float32 [10, 384], P(None, 'fsdp')
- new_qkv: float32 [384, 1152], P('fsdp')
- new_proj: float32 [384, 384], P('fsdp')
- new_fc1: float32 [384, 1536], P('fsdp')
- new_fc2: float32 [1536, 384], P(None, 'fsdp')
- new_gains: float32 [2, 384], P(None, 'fsdp')
- new_biases: float32 [10, 384], P(None, 'fsdp')
- next_mom_qkv: float32 [384, 1152], P('fsdp')
- next_mom_proj: float32 [384, 384], P('fsdp')
- next_mom_fc1: float32 [384, 1536], P('fsdp')
- next_mom_fc2: float32 [1536, 384], P(None, 'fsdp')
- next_gains_first: float32 [2, 384], P(None, 'fsdp')
- next_gains_second: float32 [2, 384], P(None, 'fsdp')
- next_biases_first: float32 [10, 384], P(None, 'fsdp')
- next_biases_second: float32 [10, 384], P(None, 'fsdp')
Inputs may be any that keep to these rules, and one draw needn't show every extreme that they name: counts[d] of device d's 16 slots, the first ones, hold images; at least one device holds 16.
All inputs are finite; a program needn't handle non-finite values.
Results may differ from a plain program's by a relative error of at most 0.0095.
The roundings to bfloat16 on the way count: a program that leaves them out, or rounds other values in their place, can miss the bound.
Values may be sent and summed in bfloat16 or wider, within the bound.
No kernel may reach another device: no remote copies, remote signals or barrier semaphores. Data moves between devices by JAX's collectives and lax.ppermute only.
A program may use at most 320 MiB of HBM per device.

v0:
```python
import math

import jax
import jax.numpy as jnp
from jax import lax
from jax.sharding import PartitionSpec as P

D = 384
H = 6
HD = 64
F = 1536
NS_ITERS = 5
ADAM_STEP = 3


NORM_EPSILON = 1e-06
ORTHO_EPSILON = 1e-07
COEFF_FIRST = 3.4445
COEFF_SECOND = -4.775
COEFF_THIRD = 2.0315
MUON_RATE = 0.3
MUON_MOMENTUM = 0.95
ADAM_RATE = 0.2
ADAM_FIRST = 0.9
ADAM_SECOND = 0.95
ADAM_EPSILON = 1e-08
ADAM_DECAY = 0.25


def layer_norm(values, gain, shift):
    centred = values - jnp.mean(values, axis=-1, keepdims=True)
    inverse = lax.rsqrt(jnp.mean(centred * centred, axis=-1, keepdims=True) + NORM_EPSILON)
    normed = centred * inverse
    return (normed * gain + shift, normed, inverse)


def norm_back(grad_out, normed, inverse, gain):
    scaled = grad_out * gain
    return inverse * (
        scaled
        - jnp.mean(scaled, axis=-1, keepdims=True)
        - normed * jnp.mean(scaled * normed, axis=-1, keepdims=True)
    )


def normal_cdf(pre_act):
    return 0.5 * (1.0 + lax.erf(pre_act * (1.0 / math.sqrt(2.0))))


def gelu_value(pre_act):
    return pre_act * normal_cdf(pre_act)


def gelu_slope(pre_act):
    density = jnp.exp(-0.5 * pre_act * pre_act) * (1.0 / math.sqrt(2.0 * math.pi))
    return normal_cdf(pre_act) + pre_act * density


def make_live(live_count, slot_count, tokens):
    live_slots = jnp.arange(slot_count, dtype=jnp.int32) < live_count
    return jnp.broadcast_to(live_slots[:, None], (slot_count, tokens)).reshape(
        slot_count * tokens, 1
    )


def forward_pass(images, live_rows, params):
    w_qkv, w_proj, w_fc1, w_fc2, gains, biases = params
    slot_count, tokens, model_width = images.shape
    row_count = slot_count * tokens
    hidden = w_fc1.shape[1]
    gain_vec = gains.astype(jnp.float32)
    shift_vec = biases.astype(jnp.float32)
    inputs = images.astype(jnp.float32).reshape(row_count, model_width)
    normed_in, norm_one, inv_one = layer_norm(inputs, gain_vec[0], shift_vec[0])
    attn_in = normed_in.astype(jnp.bfloat16)
    qkv_shift = jnp.concatenate([shift_vec[1], jnp.zeros_like(shift_vec[1]), shift_vec[2]])
    projected = (jnp.dot(attn_in, w_qkv, preferred_element_type=jnp.float32) + qkv_shift).astype(
        jnp.bfloat16
    )
    projected = projected.reshape(slot_count, tokens, 3, H, HD)
    query_h = projected[:, :, 0]
    key_h = projected[:, :, 1]
    value_h = projected[:, :, 2]
    score_scale = 1.0 / math.sqrt(HD)
    scores = (
        jnp.einsum("bshd,bthd->bhst", query_h, key_h, preferred_element_type=jnp.float32)
        * score_scale
    )
    log_total = jnp.log(jnp.sum(jnp.exp(scores), axis=-1, keepdims=True))
    probs_b = jnp.exp(scores - log_total).astype(jnp.bfloat16)
    attended = jnp.einsum("bhst,bthd->bshd", probs_b, value_h, preferred_element_type=jnp.float32)
    attended = attended.astype(jnp.bfloat16).reshape(row_count, model_width)
    residual = inputs + jnp.dot(attended, w_proj, preferred_element_type=jnp.float32) + shift_vec[3]
    normed_mid, norm_two, inv_two = layer_norm(residual, gain_vec[1], shift_vec[4])
    mlp_in = normed_mid.astype(jnp.bfloat16)
    pre_act = jnp.dot(mlp_in, w_fc1, preferred_element_type=jnp.float32) + shift_vec[6:].reshape(
        hidden
    )
    activated = gelu_value(pre_act).astype(jnp.bfloat16)
    outputs = (
        residual + jnp.dot(activated, w_fc2, preferred_element_type=jnp.float32) + shift_vec[5]
    )
    block_out = (
        jnp.where(live_rows, outputs, 0.0)
        .astype(jnp.bfloat16)
        .reshape(slot_count, tokens, model_width)
    )
    saved = (
        norm_one,
        inv_one,
        attn_in,
        query_h,
        key_h,
        value_h,
        log_total,
        attended,
        norm_two,
        inv_two,
        mlp_in,
        pre_act,
        activated,
    )
    return (block_out, saved)


def backward_pass(cotangent, live_rows, saved, params):
    w_qkv, w_proj, w_fc1, w_fc2, gains, biases = params
    (
        norm_one,
        inv_one,
        attn_in,
        query_h,
        key_h,
        value_h,
        log_total,
        attended,
        norm_two,
        inv_two,
        mlp_in,
        pre_act,
        activated,
    ) = saved
    slot_count, tokens, model_width = cotangent.shape
    row_count = slot_count * tokens
    hidden = w_fc1.shape[1]
    gain_vec = gains.astype(jnp.float32)
    out_grad = jnp.where(
        live_rows, cotangent.reshape(row_count, model_width), jnp.zeros((), jnp.bfloat16)
    )
    out_float = out_grad.astype(jnp.float32)
    grad_fc2 = jnp.dot(activated.T, out_grad, preferred_element_type=jnp.float32)
    pre_grad = jnp.dot(out_grad, w_fc2.T, preferred_element_type=jnp.float32) * gelu_slope(pre_act)
    pre_grad_b = pre_grad.astype(jnp.bfloat16)
    grad_fc1 = jnp.dot(mlp_in.T, pre_grad_b, preferred_element_type=jnp.float32)
    mid_grad = jnp.dot(pre_grad_b, w_fc1.T, preferred_element_type=jnp.float32)
    resid_grad = out_float + norm_back(mid_grad, norm_two, inv_two, gain_vec[1])
    resid_grad_b = resid_grad.astype(jnp.bfloat16)
    grad_proj = jnp.dot(attended.T, resid_grad_b, preferred_element_type=jnp.float32)
    attn_grad = jnp.dot(resid_grad_b, w_proj.T, preferred_element_type=jnp.float32).astype(
        jnp.bfloat16
    )
    attn_grad = attn_grad.reshape(slot_count, tokens, H, HD)
    score_scale = 1.0 / math.sqrt(HD)
    scores = (
        jnp.einsum("bshd,bthd->bhst", query_h, key_h, preferred_element_type=jnp.float32)
        * score_scale
    )
    attn_probs = jnp.exp(scores - log_total)
    probs_b = attn_probs.astype(jnp.bfloat16)
    value_grad = jnp.einsum(
        "bhst,bshd->bthd", probs_b, attn_grad, preferred_element_type=jnp.float32
    )
    prob_grad = jnp.einsum(
        "bshd,bthd->bhst", attn_grad, value_h, preferred_element_type=jnp.float32
    )
    inner_sum = jnp.sum(attn_probs * prob_grad, axis=-1, keepdims=True)
    score_grad = (attn_probs * (prob_grad - inner_sum) * score_scale).astype(jnp.bfloat16)
    query_grad = jnp.einsum(
        "bhst,bthd->bshd", score_grad, key_h, preferred_element_type=jnp.float32
    )
    key_grad = jnp.einsum(
        "bhst,bshd->bthd", score_grad, query_h, preferred_element_type=jnp.float32
    )
    qkv_grad = jnp.stack([query_grad, key_grad, value_grad], axis=2).reshape(
        row_count, 3 * model_width
    )
    qkv_grad_b = qkv_grad.astype(jnp.bfloat16)
    grad_qkv = jnp.dot(attn_in.T, qkv_grad_b, preferred_element_type=jnp.float32)
    in_grad = jnp.dot(qkv_grad_b, w_qkv.T, preferred_element_type=jnp.float32)
    input_grad = (resid_grad + norm_back(in_grad, norm_one, inv_one, gain_vec[0])).astype(
        jnp.bfloat16
    )
    input_grad = input_grad.reshape(slot_count, tokens, model_width)
    grad_gains = jnp.stack(
        [jnp.sum(in_grad * norm_one, axis=0), jnp.sum(mid_grad * norm_two, axis=0)]
    )
    vector_rows = jnp.stack(
        [
            jnp.sum(in_grad, axis=0),
            jnp.sum(query_grad.reshape(row_count, model_width), axis=0),
            jnp.sum(value_grad.reshape(row_count, model_width), axis=0),
            jnp.sum(resid_grad, axis=0),
            jnp.sum(mid_grad, axis=0),
            jnp.sum(out_float, axis=0),
        ]
    )
    grad_biases = jnp.concatenate(
        [vector_rows, jnp.sum(pre_grad, axis=0).reshape(hidden // model_width, model_width)], axis=0
    )
    return (input_grad, (grad_qkv, grad_proj, grad_fc1, grad_fc2, grad_gains, grad_biases))


def orthogonalize(matrix):
    norm_value = jnp.sqrt(jnp.sum(matrix * matrix))
    current = matrix / (norm_value + ORTHO_EPSILON)
    for iteration in range(NS_ITERS):
        square = jnp.dot(current, current.T, precision=lax.Precision.HIGHEST)
        polynomial = COEFF_SECOND * square + COEFF_THIRD * jnp.dot(
            square, square, precision=lax.Precision.HIGHEST
        )
        current = COEFF_FIRST * current + jnp.dot(
            polynomial, current, precision=lax.Precision.HIGHEST
        )
    return current


def adam_update(parameter, gradient, first_state, second_state):
    next_first = ADAM_FIRST * first_state + (1.0 - ADAM_FIRST) * gradient
    next_second = ADAM_SECOND * second_state + (1.0 - ADAM_SECOND) * gradient * gradient
    first_hat = next_first / (1.0 - ADAM_FIRST**ADAM_STEP)
    second_hat = next_second / (1.0 - ADAM_SECOND**ADAM_STEP)
    updated = parameter - ADAM_RATE * (
        first_hat / (jnp.sqrt(second_hat) + ADAM_EPSILON) + ADAM_DECAY * parameter
    )
    return (updated, next_first, next_second)


def muon_factor(row_total, column_total):
    return math.sqrt(max(1.0, row_total / column_total))


def body(
    images,
    cotangent,
    counts,
    w_qkv,
    w_proj,
    w_fc1,
    w_fc2,
    gains,
    biases,
    mom_qkv,
    mom_proj,
    mom_fc1,
    mom_fc2,
    gains_first,
    gains_second,
    biases_first,
    biases_second,
):
    slot_count, tokens, model_width = images.shape
    live_rows = make_live(counts[0], slot_count, tokens)
    shard_params = (
        w_qkv.astype(jnp.bfloat16),
        w_proj.astype(jnp.bfloat16),
        w_fc1.astype(jnp.bfloat16),
        w_fc2.astype(jnp.bfloat16),
        gains.astype(jnp.bfloat16),
        biases.astype(jnp.bfloat16),
    )
    full_params = (
        lax.all_gather(shard_params[0], "fsdp", axis=0, tiled=True),
        lax.all_gather(shard_params[1], "fsdp", axis=0, tiled=True),
        lax.all_gather(shard_params[2], "fsdp", axis=0, tiled=True),
        lax.all_gather(shard_params[3], "fsdp", axis=1, tiled=True),
        lax.all_gather(shard_params[4], "fsdp", axis=1, tiled=True),
        lax.all_gather(shard_params[5], "fsdp", axis=1, tiled=True),
    )
    block_out, saved = forward_pass(images, live_rows, full_params)
    back_params = (
        lax.all_gather(shard_params[0], "fsdp", axis=0, tiled=True),
        lax.all_gather(shard_params[1], "fsdp", axis=0, tiled=True),
        lax.all_gather(shard_params[2], "fsdp", axis=0, tiled=True),
        lax.all_gather(shard_params[3], "fsdp", axis=1, tiled=True),
        lax.all_gather(shard_params[4], "fsdp", axis=1, tiled=True),
        lax.all_gather(shard_params[5], "fsdp", axis=1, tiled=True),
    )
    input_grad, local_grads = backward_pass(cotangent, live_rows, saved, back_params)
    group_sums = (
        lax.psum_scatter(local_grads[0], "fsdp", scatter_dimension=0, tiled=True),
        lax.psum_scatter(local_grads[1], "fsdp", scatter_dimension=0, tiled=True),
        lax.psum_scatter(local_grads[2], "fsdp", scatter_dimension=0, tiled=True),
        lax.psum_scatter(local_grads[3], "fsdp", scatter_dimension=1, tiled=True),
        lax.psum_scatter(local_grads[4], "fsdp", scatter_dimension=1, tiled=True),
        lax.psum_scatter(local_grads[5], "fsdp", scatter_dimension=1, tiled=True),
    )
    summed = lax.psum(
        (group_sums[0], group_sums[1], group_sums[2], group_sums[3], group_sums[4], group_sums[5]),
        "rep",
    )
    device_total = lax.axis_size("rep") * lax.axis_size("fsdp")
    grad_qkv, grad_proj, grad_fc1, grad_fc2, grad_gains, grad_biases = tuple(
        (item / device_total for item in summed)
    )
    next_qkv = MUON_MOMENTUM * mom_qkv + grad_qkv
    next_proj = MUON_MOMENTUM * mom_proj + grad_proj
    next_fc1 = MUON_MOMENTUM * mom_fc1 + grad_fc1
    next_fc2 = MUON_MOMENTUM * mom_fc2 + grad_fc2
    width_part = next_qkv.shape[0]
    full_qkv, full_proj, full_fc1, full_fc2 = (
        lax.all_gather(next_qkv, "fsdp", axis=0, tiled=True),
        lax.all_gather(next_proj, "fsdp", axis=0, tiled=True),
        lax.all_gather(next_fc1, "fsdp", axis=0, tiled=True),
        lax.all_gather(next_fc2, "fsdp", axis=1, tiled=True),
    )
    start_row = lax.axis_index("fsdp") * width_part
    orth_qkv = lax.dynamic_slice_in_dim(orthogonalize(full_qkv), start_row, width_part, 0)
    orth_proj = lax.dynamic_slice_in_dim(orthogonalize(full_proj), start_row, width_part, 0)
    orth_fc1 = lax.dynamic_slice_in_dim(orthogonalize(full_fc1), start_row, width_part, 0)
    orth_fc2 = lax.dynamic_slice_in_dim(orthogonalize(full_fc2.T), start_row, width_part, 0).T
    new_qkv = w_qkv - MUON_RATE * muon_factor(D, 3 * D) * orth_qkv
    new_proj = w_proj - MUON_RATE * muon_factor(D, D) * orth_proj
    new_fc1 = w_fc1 - MUON_RATE * muon_factor(D, F) * orth_fc1
    new_fc2 = w_fc2 - MUON_RATE * muon_factor(F, D) * orth_fc2
    new_gains, next_gains_first, next_gains_second = adam_update(
        gains, grad_gains, gains_first, gains_second
    )
    new_biases, next_biases_first, next_biases_second = adam_update(
        biases, grad_biases, biases_first, biases_second
    )
    return (
        block_out,
        input_grad,
        grad_qkv,
        grad_proj,
        grad_fc1,
        grad_fc2,
        grad_gains,
        grad_biases,
        new_qkv,
        new_proj,
        new_fc1,
        new_fc2,
        new_gains,
        new_biases,
        next_qkv,
        next_proj,
        next_fc1,
        next_fc2,
        next_gains_first,
        next_gains_second,
        next_biases_first,
        next_biases_second,
    )


def solution(mesh):
    in_specs = (
        P(("rep", "fsdp"), None, None),
        P(("rep", "fsdp"), None, None),
        P(("rep", "fsdp")),
        P("fsdp", None),
        P("fsdp", None),
        P("fsdp", None),
        P(None, "fsdp"),
        P(None, "fsdp"),
        P(None, "fsdp"),
        P("fsdp", None),
        P("fsdp", None),
        P("fsdp", None),
        P(None, "fsdp"),
        P(None, "fsdp"),
        P(None, "fsdp"),
        P(None, "fsdp"),
        P(None, "fsdp"),
    )
    out_specs = (
        P(("rep", "fsdp"), None, None),
        P(("rep", "fsdp"), None, None),
        P("fsdp", None),
        P("fsdp", None),
        P("fsdp", None),
        P(None, "fsdp"),
        P(None, "fsdp"),
        P(None, "fsdp"),
        P("fsdp", None),
        P("fsdp", None),
        P("fsdp", None),
        P(None, "fsdp"),
        P(None, "fsdp"),
        P(None, "fsdp"),
        P("fsdp", None),
        P("fsdp", None),
        P("fsdp", None),
        P(None, "fsdp"),
        P(None, "fsdp"),
        P(None, "fsdp"),
        P(None, "fsdp"),
        P(None, "fsdp"),
    )
    return jax.shard_map(body, mesh=mesh, in_specs=in_specs, out_specs=out_specs, check_vma=False)
```

profile of v0, /device:TPU:0, one launch (start us, length us, event | category | flops | bytes accessed | tf_op | source)
XLA Modules:
  0.0 869.8 jit_solution(7720072122847908127)
XLA Ops:
  29.8 10.0 %all_gather.37 = bf16[384,1152]{1,0:T(8,128)(2,1)} all-gather(bf16[96,1152]{1,0:T(8,128)(2,1)S(1)} %convert_element_type.98), channel_id=1, replica_groups=mesh['rep'=8,'fsdp'=4] {'fsdp'}, dimensions={0}, use_global_device_ids=true | all-gather | bytes 1105920 | tf_op jit(solution)/shard_map/all_gather | solution.py:272
  54.5 22.3 %reshape.200 = bf16[16,197,3,6,64]{4,3,2,1,0:T(8,128)(2,1)} reshape(bf16[3152,1152]{1,0:T(8,128)(2,1)} %fusion.11) | data formatting | bytes 14524416 | tf_op jit(solution)/shard_map/reshape | solution.py:80
  76.8 15.3 %fusion.116 = (bf16[16,197,1,6,64]{4,3,2,1,0:T(8,128)(2,1)}, bf16[16,197,1,6,64]{4,3,2,1,0:T(8,128)(2,1)}, bf16[16,197,1,6,64]{4,3,2,1,0:T(8,128)(2,1)}) fusion(bf16[16,197,3,6,64]{4,3,2,1,0:T(8,128)(2,1)} %reshape.200), kind=kLoop, calls=%fused_computation.213 | loop fusion | bytes 14524416 | tf_op jit(solution)/shard_map/slice | solution.py:81
  116.1 12.3 %fusion.38 = f32[16,6,197,197]{2,3,1,0:T(8,128)} fusion(bf16[16,197,1,6,64]{1,4,3,0,2:T(8,128)(2,1)} %copy.134, bf16[16,197,1,6,64]{1,4,3,0,2:T(8,128)(2,1)} %copy.133), kind=kOutput, calls=%fused_computation.65 | convolution fusion | flops 476884992 | bytes 19744128 | tf_op jit(solution)/shard_map/bshd,bthd->bhst/dot_general | solution.py:86
  128.4 22.3 %fusion.2 = f32[16,6,197,197]{2,3,1,0:T(8,128)} fusion(f32[16,6,197,197]{2,3,1,0:T(8,128)} %fusion.38), kind=kOutput, calls=%fused_computation.4 | output fusion | flops 11196100 | bytes 29805312 | tf_op jit(solution)/shard_map/reduce_sum | solution.py:89
  150.7 18.7 %convert_bitcast_fusion = bf16[16,197,6,64]{1,3,2,0:T(8,128)(2,1)} fusion(bf16[16,197,1,6,64]{1,4,3,0,2:T(8,128)(2,1)} %copy.132, f32[16,6,197,197]{2,3,1,0:T(8,128)} %fusion.38), kind=kOutput, calls=%fused_computation.72 | convolution fusion | flops 493017120 | bytes 19744128 | tf_op jit(solution)/shard_map/bhst,bthd->bshd/dot_general | solution.py:91
  207.7 13.9 %multiply_convert_fusion.1 = (bf16[3152,1536]{1,0:T(8,128)(2,1)}, f32[3152,1536]{1,0:T(8,128)}) fusion(f32[1536]{0:T(1024)S(1)} %add.318, bf16[384,1536]{1,0:T(8,128)(2,1)} %all-gather.8.cloned.1.call-done, f32[3152,384]{1,0:T(8,128)} %copy-done.1, f32[384]{0:T(512)S(1)} %get-tuple-element.119, f32[384]{0:T(512)S(1)} %get-tuple-element.124, ...), kind=kOutput, calls=%fused_computation.16 | convolution fusion | flops 3753351168 | bytes 35104384 | tf_op jit(solution)/shard_map/dot_general | solution.py:96
  221.5 16.6 %fusion.122 = (f32[1536]{0:T(1024)S(1)}, bf16[3152,1536]{1,0:T(8,128)(2,1)S(1)}) fusion(f32[3152,1536]{1,0:T(8,128)} %get-tuple-element.156, f32[1536]{0:T(1024)S(1)} %add.318, bf16[1536,384]{0,1:T(8,128)(2,1)} %all-gather.10.cloned.1.call-done, bf16[3152,384]{1,0:T(8,128)(2,1)S(1)} %copy-done.6, pred[3152]{0:T(1024)(128)(4,1)S(1)} %broadcast_in_dim.49), kind=kOutput, calls=%fused_computation.215 | convolution fusion | flops 3777556992 | bytes 32664656 | tf_op jit(solution)/shard_map/dot_general | solution.py:152
  264.9 18.7 %bitcast_reduce_fusion = (f32[6,64]{1,0:T(8,128)S(1)}, bf16[16,6,64,197]{3,2,1,0:T(8,128)(2,1)}) fusion(bf16[16,197,6,64]{1,3,2,0:T(8,128)(2,1)} %copy.110, f32[16,6,197,197]{2,3,1,0:T(8,128)} %fusion.38), kind=kOutput, calls=%fused_computation.26 | convolution fusion | flops 494227104 | bytes 19745664 | tf_op jit(solution)/shard_map/bhst,bshd->bthd/dot_general | solution.py:170
  283.6 11.3 %fusion.42 = f32[16,6,197,197]{2,3,1,0:T(8,128)} fusion(bf16[16,197,6,64]{1,3,2,0:T(8,128)(2,1)} %copy.110, bf16[16,197,1,6,64]{1,4,3,0,2:T(8,128)(2,1)S(1)} %copy-done.4), kind=kOutput, calls=%fused_computation.69 | convolution fusion | flops 476884992 | bytes 19744128 | tf_op jit(solution)/shard_map/bshd,bthd->bhst/dot_general | solution.py:173
  294.9 28.1 %fusion.45 = bf16[16,197,1,6,64]{1,4,3,0,2:T(8,128)(2,1)} fusion(f32[16,6,197,197]{2,3,1,0:T(8,128)} %fusion.2, f32[16,6,197,197]{2,3,1,0:T(8,128)} %fusion.42, bf16[16,197,1,6,64]{1,4,3,0,2:T(8,128)(2,1)} %copy.133), kind=kOutput, calls=%fused_computation.81 | convolution fusion | flops 495532416 | bytes 34646784 | tf_op jit(solution)/shard_map/bhst,bshd->bthd/dot_general | solution.py:181
  323.1 28.8 %bitcast_reduce_fusion.1 = (f32[6,64]{1,0:T(8,128)S(1)}, bf16[16,6,64,197]{3,2,1,0:T(8,128)(2,1)}) fusion(f32[16,6,197,197]{2,3,1,0:T(8,128)} %fusion.2, f32[16,6,197,197]{2,3,1,0:T(8,128)} %fusion.42, bf16[16,197,1,6,64]{1,4,3,0,2:T(8,128)(2,1)} %copy.134), kind=kOutput, calls=%fused_computation.27 | convolution fusion | flops 497952768 | bytes 34648320 | tf_op jit(solution)/shard_map/bhst,bthd->bshd/dot_general | solution.py:178
  366.0 14.0 %copy.115 = bf16[16,197,3,6,64]{1,0,4,3,2:T(8,128)(2,1)} copy(bf16[16,197,3,6,64]{1,4,3,0,2:T(8,128)(2,1)} %maximum_convert_fusion) | data formatting | bytes 14524416 | tf_op jit(solution)/shard_map/convert_element_type | solution.py:187
  379.9 19.0 %convert_element_type.115 = bf16[3152,1152]{0,1:T(8,128)(2,1)} reshape(bf16[16,197,3,6,64]{1,0,4,3,2:T(8,128)(2,1)} %copy.115) | data formatting | bytes 14524416 | tf_op jit(solution)/shard_map/convert_element_type | solution.py:187
  406.8 11.1 %fusion.33 = f32[384,1536]{1,0:T(8,128)} fusion(bf16[3152,1536]{1,0:T(8,128)(2,1)} %copy-done.42, f32[3152,384]{1,0:T(8,128)} %copy-done.1, f32[384]{0:T(512)S(1)} %get-tuple-element.119, f32[384]{0:T(512)S(1)} %get-tuple-element.124, f32[3152]{0:T(1024)S(1)} %add_rsqrt_fusion, f32[3152]{0:T(1024)S(1)} %broadcast_multiply_fusion.8), kind=kOutput, calls=%fused_computation.47 | convolution fusion | flops 3724302336 | bytes 16912000 | tf_op jit(solution)/shard_map/dot_general | solution.py:154
  417.9 9.4 %fusion.113 = f32[1536,384]{0,1:T(8,128)} fusion(bf16[3152,1536]{1,0:T(8,128)(2,1)} %get-tuple-element.155, bf16[3152,384]{1,0:T(8,128)(2,1)S(1)} %copy-done.7, pred[3152]{0:T(1024)(128)(4,1)S(1)} %broadcast_in_dim.49), kind=kOutput, calls=%fused_computation.210 | convolution fusion | flops 3719460864 | bytes 14466128 | tf_op jit(solution)/shard_map/dot_general | solution.py:151
  427.4 9.9 %reduce-scatter.11.cloned.1.call-done = f32[96,1152]{1,0:T(8,128)} async-done(((f32[384,1152]{1,0:T(8,128)}), f32[96,1152]{1,0:T(8,128)}) %reduce-scatter.11.cloned.1.call-update) | async-done | bytes 442384 | tf_op jit(solution)/shard_map/reduce_scatter | solution.py:290
  437.4 35.8 %reduce-scatter.15.cloned.1.call-done = f32[96,1536]{1,0:T(8,128)} async-done(((f32[384,1536]{1,0:T(8,128)}), f32[96,1536]{1,0:T(8,128)}) %reduce-scatter.15.cloned.1.call-update) | async-done | bytes 589840 | tf_op jit(solution)/shard_map/reduce_scatter | solution.py:292
  473.2 35.8 %reduce-scatter.17.cloned.1.call-done = f32[1536,96]{0,1:T(8,128)} async-done(((f32[1536,384]{0,1:T(8,128)}), f32[1536,96]{0,1:T(8,128)}) %reduce-scatter.17.cloned.1.call-update) | async-done | bytes 589840 | tf_op jit(solution)/shard_map/reduce_scatter | solution.py:293
  510.2 12.1 %multiply_reduce_fusion.2 = (f32[384]{0:T(512)S(1)}, f32[3152]{0:T(1024)S(1)}, f32[3152]{0:T(1024)S(1)}, f32[384]{0:T(512)S(1)}, f32[3152,384]{1,0:T(8,128)}) fusion(f32[3152,384]{1,0:T(8,128)} %reshape.182, f32[3152]{0:T(1024)S(1)} %copy-done.30, f32[3152]{0:T(1024)S(1)} %copy-done.28, f32[384]{0:T(512)S(1)} %get-tuple-element.125, ...), kind=kOutput, calls=%fused_computation.41 | convolution fusion | flops 2799574016 | bytes 17884928 | tf_op jit(solution)/shard_map/dot_general | solution.py:189
  524.5 10.3 %fusion.28 = bf16[3152,384]{1,0:T(8,128)(2,1)} fusion(f32[3152,384]{1,0:T(8,128)} %copy-done.1, bf16[3152,1536]{1,0:T(8,128)(2,1)} %get-tuple-element.155, bf16[1536,384]{0,1:T(8,128)(2,1)S(1)} %copy-done.40, f32[384]{0:T(512)S(1)} %copy-done.35, pred[3152]{0:T(1024)(128)(4,1)S(1)} %broadcast_in_dim.49), kind=kOutput, calls=%fused_computation.34 | convolution fusion | flops 3723091968 | bytes 18129488 | tf_op jit(solution)/shard_map/dot_general | solution.py:101
  534.8 72.0 %all-reduce.4.cloned.1.call-done = (f32[96,1152]{1,0:T(8,128)}, f32[96,384]{1,0:T(8,128)}, f32[96,1536]{1,0:T(8,128)}, f32[1536,96]{0,1:T(8,128)}) async-done(((f32[96,1152]{1,0:T(8,128)}, f32[96,384]{1,0:T(8,128)}, f32[96,1536]{1,0:T(8,128)}, f32[1536,96]{0,1:T(8,128)}), (f32[96,1152]{1,0:T(8,128)}, f32[96,384]{1,0:T(8,128)}, f32[96,1536]{1,0:T(8,128)}, f32[1536,96]{0,1:T(8,128)})) %all-reduce.4.cloned.1.call-update) | async-done | bytes 1769488 | tf_op jit(solution)/shard_map/psum | solution.py:297
  629.9 22.0 %reduce-scatter.21.cloned.1.call-done = f32[96,10]{1,0:T(8,128)} async-done(((f32[384,10]{1,0:T(8,128)}), f32[96,10]{1,0:T(8,128)}) %reduce-scatter.21.cloned.1.call-update) | async-done | bytes 3856
  652.7 21.9 %all-reduce = (f32[2,96]{1,0:T(2,128)S(1)}, f32[10,96]{1,0:T(8,128)S(1)}) all-reduce(f32[2,96]{1,0:T(2,128)S(1)} %copy.125, f32[10,96]{1,0:T(8,128)S(1)} %copy.127), channel_id=1, replica_groups=mesh['rep'=8,'fsdp'=4] {'rep'}, use_global_device_ids=true, to_apply=%region_21.22 | all-reduce | flops 1152 | bytes 9216 | tf_op jit(solution)/shard_map/psum | solution.py:297
  (278 shorter events, 359.1 us)
Async XLA Ops:
  7.2 200.5 %all-gather.8.cloned.1.call-start = ((), (), s32[]{:S(2)}) async-start(), calls=%async_computation.6 | async-start | bytes 1474560 | tf_op jit(solution)/shard_map/all_gather | solution.py:274
  9.1 212.4 %all-gather.10.cloned.1.call-start = ((), (), s32[]{:S(2)}) async-start(), calls=%async_computation.7 | async-start | bytes 1474560 | tf_op jit(solution)/shard_map/all_gather | solution.py:275
  11.0 416.5 %reduce-scatter.13.cloned.1.call-start = ((), (), s32[]{:S(2)}) async-start(), calls=%async_computation.9 | async-start | bytes 737280 | tf_op jit(solution)/shard_map/reduce_scatter | solution.py:291
  356.5 80.8 %reduce-scatter.11.cloned.1.call-start = ((), (), s32[]{:S(2)}) async-start(), calls=%async_computation.8 | async-start | bytes 2211840 | tf_op jit(solution)/shard_map/reduce_scatter | solution.py:290
  406.7 66.4 %reduce-scatter.15.cloned.1.call-start = ((), (), s32[]{:S(2)}) async-start(), calls=%async_computation.10 | async-start | bytes 2949120 | tf_op jit(solution)/shard_map/reduce_scatter | solution.py:292
  417.9 91.1 %reduce-scatter.17.cloned.1.call-start = ((), (), s32[]{:S(2)}) async-start(), calls=%async_computation.11 | async-start | bytes 2949120 | tf_op jit(solution)/shard_map/reduce_scatter | solution.py:293
  427.3 82.1 %copy-start.5 = (bf16[16,197,384]{2,0,1:T(8,128)(2,1)S(1)}, bf16[16,197,384]{2,0,1:T(8,128)(2,1)}, u32[]{:S(2)}) copy-start(bf16[16,197,384]{2,0,1:T(8,128)(2,1)} %param.18) | copy-start | bytes 7262212
  427.3 82.9 %copy-start.16 = (bf16[384,1152]{1,0:T(8,128)(2,1)S(1)}, bf16[384,1152]{1,0:T(8,128)(2,1)}, u32[]{:S(2)}) copy-start(bf16[384,1152]{1,0:T(8,128)(2,1)} %all_gather.37) | copy-start | bytes 2654212
  427.3 82.9 %copy-start.28 = (f32[3152]{0:T(1024)S(1)}, f32[3152]{0:T(1024)}, u32[]{:S(2)}) copy-start(f32[3152]{0:T(1024)} %copy-done.27) | copy-start | bytes 37828
  427.3 82.9 %copy-start.30 = (f32[3152]{0:T(1024)S(1)}, f32[3152]{0:T(1024)}, u32[]{:S(2)}) copy-start(f32[3152]{0:T(1024)} %copy-done.29) | copy-start | bytes 37828
  427.4 179.5 %all-reduce.4.cloned.1.call-start = ((), (), s32[]{:S(2)}) async-start(), calls=%async_computation.17 | async-start | bytes 3538944 | tf_op jit(solution)/shard_map/psum | solution.py:297
  509.0 120.0 %reduce-scatter.19.cloned.1.call-start = ((), (), s32[]{:S(2)}) async-start(), calls=%async_computation.15 | async-start | bytes 245760
  523.2 128.7 %reduce-scatter.21.cloned.1.call-start = ((), (), s32[]{:S(2)}) async-start(), calls=%async_computation.16 | async-start | bytes 245760
  524.4 183.0 %all-gather.12.cloned.1.call-start = ((), (), s32[]{:S(2)}) async-start(), calls=%async_computation.12 | async-start | bytes 2211840 | tf_op jit(solution)/shard_map/all_gather | solution.py:311
  524.5 82.3 %copy-start.24 = (f32[96,1152]{1,0:T(8,128)S(1)}, f32[96,1152]{1,0:T(8,128)}, u32[]{:S(2)}) copy-start(f32[96,1152]{1,0:T(8,128)} %param.26) | copy-start | bytes 1327108
  608.8 144.4 %all-gather.14.cloned.1.call-start = ((), (), s32[]{:S(2)}) async-start(), calls=%async_computation.13 | async-start | bytes 2949120 | tf_op jit(solution)/shard_map/all_gather | solution.py:313
  622.7 51.9 %copy-start.37 = (f32[2,96]{1,0:T(2,128)S(1)}, f32[2,96]{1,0:T(2,128)}, u32[]{:S(2)}) copy-start(f32[2,96]{1,0:T(2,128)} %param.24) | copy-start | bytes 2308
  622.8 51.9 %copy-start.38 = (f32[2,96]{1,0:T(2,128)S(1)}, f32[2,96]{1,0:T(2,128)}, u32[]{:S(2)}) copy-start(f32[2,96]{1,0:T(2,128)} %param.30) | copy-start | bytes 2308
  622.8 52.5 %copy-start.32 = (f32[10,96]{1,0:T(8,128)S(1)}, f32[10,96]{1,0:T(8,128)}, u32[]{:S(2)}) copy-start(f32[10,96]{1,0:T(8,128)} %param.25) | copy-start | bytes 11524
  622.8 52.4 %copy-start.33 = (f32[10,96]{1,0:T(8,128)S(1)}, f32[10,96]{1,0:T(8,128)}, u32[]{:S(2)}) copy-start(f32[10,96]{1,0:T(8,128)} %param.32) | copy-start | bytes 11524
  622.8 52.4 %copy-start.34 = (f32[10,96]{1,0:T(8,128)S(1)}, f32[10,96]{1,0:T(8,128)}, u32[]{:S(2)}) copy-start(f32[10,96]{1,0:T(8,128)} %param.33) | copy-start | bytes 11524
  622.8 53.1 %copy-start.25 = (f32[96,384]{1,0:T(8,128)S(1)}, f32[96,384]{1,0:T(8,128)}, u32[]{:S(2)}) copy-start(f32[96,384]{1,0:T(8,128)} %param.27) | copy-start | bytes 442372
  622.8 53.0 %copy-start.26 = (f32[96,384]{1,0:T(8,128)S(1)}, f32[96,384]{1,0:T(8,128)}, u32[]{:S(2)}) copy-start(f32[96,384]{1,0:T(8,128)} %get-tuple-element.129) | copy-start | bytes 442372
  691.0 117.2 %all-gather.16.cloned.1.call-start = ((), (), s32[]{:S(2)}) async-start(), calls=%async_computation.14 | async-start | bytes 2949120 | tf_op jit(solution)/shard_map/all_gather | solution.py:314
  (33 other events, 401.4 us)
Sparse Core Ops, SparseCore 0:
  10.1 20.1 all-gather.7
  32.5 17.4 all-gather.9
  356.7 23.3 reduce-scatter.12
  406.8 30.4 reduce-scatter.10
  440.3 32.8 reduce-scatter.14
  476.1 32.8 reduce-scatter.16
  512.9 93.8 all-reduce.3
  609.8 19.1 reduce-scatter.18
  632.1 19.7 reduce-scatter.20
  653.9 20.7 all-gather.11
  691.1 21.1 all-gather.13
  714.3 24.0 all-gather.15
where the time goes:
time: 876 us; the launch traced here: 870 us
  matrix products  387 us (44%)
  waiting for transfers between devices  180 us (21%)
  local copies, waits for them, and re-layouts  156 us (18%)
  other arithmetic  70.7 us (8%)
  blocking collectives  56.2 us (6%)
  between operations  19.3 us (2%)
    psum x1, waiting for transfers between devices, body(): lax.psum((group_sums[0], group_sums[1], group_sums[2], group_sums[3], gro...  72 us
    dot_general x20, matrix products, orthogonalize(): square = jnp.dot(current, current.T, precision=lax.Precision.HIGHEST)  70.7 us
    dot_general x20, matrix products, orthogonalize(): jnp.dot(polynomial, current, precision=lax.Precision.HIGHEST)  63.7 us
    unnamed x100, local copies, waits for them, and re-layouts  39.3 us
    reduce_scatter x1, waiting for transfers between devices, body(): lax.psum_scatter(local_grads[3], 'fsdp', scatter_dimension=1, tiled=True)  35.8 us
    reduce_scatter x1, waiting for transfers between devices, body(): lax.psum_scatter(local_grads[2], 'fsdp', scatter_dimension=0, tiled=True)  35.8 us
    convert_element_type x2, local copies, waits for them, and re-layouts, backward_pass(): qkv_grad_b = qkv_grad.astype(jnp.bfloat16)  32.9 us
    dot_general x1, matrix products, backward_pass(): jnp.einsum('bhst,bthd->bshd', score_grad, key_h, preferred_element_type=j...  28.8 us
  transfers between devices with their start and end apart: 12, of which 6 were waited for; matrix products, arithmetic and copies ran while one was open for 48% of the time, Pallas kernels for 0%

commit v1 on v0

v1 whole, which is shorter than its diff:
```python
import math

import jax
import jax.numpy as jnp
from jax import lax
from jax.experimental import pallas as pl
from jax.experimental.pallas import tpu as pltpu
from jax.sharding import PartitionSpec as P


NS_ITERS = 5
ADAM_STEP = 3
ORTHO_EPSILON = 1e-07
COEFF_FIRST = 3.4445
COEFF_SECOND = -4.775
COEFF_THIRD = 2.0315
MUON_RATE = 0.3
MUON_MOMENTUM = 0.95
ADAM_RATE = 0.2
ADAM_FIRST = 0.9
ADAM_SECOND = 0.95
ADAM_EPSILON = 1e-08
ADAM_DECAY = 0.25

D = 384
H = 6
HD = 64
F = 1536
T = 197
TP = 208
TC = T // 16 * 16
EPS = 1e-6
NV = 12
Q_COLS = 3 * D + 128
R_COLS = D + 2 * F
F2 = F // 2
M_HALF = 256 + F
Q_HALF = Q_COLS // 2
f32 = jnp.float32
bf16 = jnp.bfloat16
SCALE = 1.0 / math.sqrt(HD)
SCALE_LOG2E = SCALE * math.log2(math.e)
VMEM_LIMIT = 60 * 1024 * 1024
S = jax.ShapeDtypeStruct
ANY = pl.BlockSpec(memory_space=pl.ANY)


def dot(a, b):
    return jnp.dot(a, b, preferred_element_type=f32)


def dot_nt(a, b):
    return lax.dot_general(a, b, (((1,), (1,)), ((), ())), preferred_element_type=f32)


def dot_tn(a, b):
    return lax.dot_general(a, b, (((0,), (0,)), ((), ())), preferred_element_type=f32)


def norm(x):
    xc = x - jnp.mean(x, axis=-1, keepdims=True)
    r = lax.rsqrt(jnp.mean(xc * xc, axis=-1, keepdims=True) + EPS)
    return xc * r, r


def norm_back(e, n, r):
    return r * (e - jnp.mean(e, axis=-1, keepdims=True) - n * jnp.mean(e * n, axis=-1, keepdims=True))


def col8(v):
    return jnp.sum(v.reshape(v.shape[0] // 8, 8, v.shape[1]), axis=0)


def total(v):
    return jnp.sum(v, axis=0, keepdims=True)


PHI_T = 0.28
PHI_C = (0.11652077999788102, 0.06749674653879187, 0.2689101818992952,
         -0.2369935012534717, 0.38987403003604115, -0.10580824648054844)
HALF_LOG2E = -0.5 * math.log2(math.e)
DENSITY = 1.0 / math.sqrt(2.0 * math.pi)


def gelu_parts(z):
    t = 1.0 / (1.0 + PHI_T * jnp.abs(z))
    bell = jnp.exp2((z * z) * HALF_LOG2E)
    poly = PHI_C[5] * t + PHI_C[4]
    for k in (3, 2, 1, 0):
        poly = poly * t + PHI_C[k]
    tail = (poly * t) * bell
    cdf = jnp.where(z < 0.0, tail, 1.0 - tail)
    return z * cdf, cdf + (z * DENSITY) * bell


def slot_of(n_ref):
    i = pl.program_id(0)
    return jnp.where(i < n_ref[1], 2 * i, 2 * (i - n_ref[1]) + 1)


def fill_pool(own_ref, got_ref, pool):
    rows = own_ref.shape[0]
    odd = lax.broadcasted_iota(jnp.int32, (rows, 128), 0) & 1
    for j in range(D // 128):
        cols = slice(128 * j, 128 * j + 128)
        pool[j, :rows] = jnp.where(odd == 0, own_ref[:, cols].astype(f32), got_ref[:, cols].astype(f32))
        pool[j, rows:] = jnp.zeros((pool.shape[1] - rows, 128), f32)


def load_image(n_ref, pool):
    rows = pl.ds(slot_of(n_ref), TP, stride=pool.shape[1] // TP)
    return jnp.concatenate([pool[j, rows, :] for j in range(D // 128)], axis=1)


def store_image(n_ref, pool, value):
    rows = pl.ds(slot_of(n_ref), TP, stride=pool.shape[1] // TP)
    for j in range(D // 128):
        pool[j, rows, :] = value[:, 128 * j : 128 * j + 128]


def empty_pool(pool, out_ref):
    for j in range(D // 128):
        out_ref[:, 128 * j : 128 * j + 128] = pool[j, : out_ref.shape[0]].astype(bf16)


def fetch(n_ref, pieces, buf, sems):
    rows = pieces[0].shape[0]
    copies = []
    for k, piece in enumerate(pieces):
        at = pl.multiple_of((n_ref[2] ^ k) * rows, 32)
        copies.append(pltpu.make_async_copy(piece, buf.at[pl.ds(at, rows)], sems.at[k]))
    for c in copies:
        c.start()
    for c in copies:
        c.wait()


def flush(n_ref, acc, send_ref, keep_ref):
    pairs, rows = keep_ref.shape[0], keep_ref.shape[1]
    me = n_ref[2] & 1
    for y in range(pairs):
        mine = pl.multiple_of((2 * y + me) * rows, 32)
        theirs = pl.multiple_of((2 * y + 1 - me) * rows, 32)
        keep_ref[y] = acc[pl.ds(mine, rows), :]
        send_ref[y] = acc[pl.ds(theirs, rows), :].astype(bf16)


def live_step(n_ref, step):
    pl.when(pl.program_id(0) < n_ref[0])(step)


def attn_fwd_kernel(parts, n_ref, xo_ref, xg_ref, *rest):
    pieces = rest[:parts]
    x_ref, qkv_ref, o_ref, lse_ref, vec_ref, w, pool, sems = rest[parts:]

    @pl.when(pl.program_id(0) == 0)
    def _():
        fetch(n_ref, pieces, w, sems)
        vec_ref[...] = w[:, 3 * D :].astype(f32).T[:16]
        fill_pool(xo_ref, xg_ref, pool)

    def step():
        x = load_image(n_ref, pool)
        x_ref[0] = x.astype(bf16)
        n1, _ = norm(x)
        a = (n1 * vec_ref[0:1] + vec_ref[2:3]).astype(bf16)
        qb = jnp.concatenate([vec_ref[3:4], jnp.zeros((1, D), f32), vec_ref[4:5]], axis=1)
        qkv = (dot(a, w[:, : 3 * D]) + qb).astype(bf16)
        real = lax.broadcasted_iota(jnp.int32, (TP - TC, 3 * D), 0) < T - TC
        qkv_ref[0, :TC] = qkv[:TC]
        qkv_ref[0, TC:] = jnp.where(real, qkv[TC:], jnp.zeros_like(qkv[TC:]))
        lane = lax.broadcasted_iota(jnp.int32, (TP, 128), 1)
        low = lane < HD
        key = lax.broadcasted_iota(jnp.int32, (TP, TP), 1) < T
        lse = jnp.zeros((TP, 128), f32)
        for pair in range(H // 2):
            at = pair * 128
            q, k, v = (qkv_ref[0, :, off + at : off + at + 128] for off in (0, D, 2 * D))
            zero = jnp.zeros_like(q)
            o = None
            for side in range(2):
                sel = low if side == 0 else jnp.logical_not(low)
                s = jnp.where(key, dot_nt(jnp.where(sel, q, zero), k) * SCALE_LOG2E, -1e30)
                l2 = jnp.log2(jnp.sum(jnp.exp2(s), axis=-1, keepdims=True))
                p = jnp.exp2(s - l2).astype(bf16)
                part = dot(p, jnp.where(sel, v, zero))
                o = part if o is None else o + part
                lse = jnp.where(lane == pair * 2 + side, l2, lse)
            o_ref[0, :, at : at + 128] = o.astype(bf16)
        lse_ref[0] = lse

    live_step(n_ref, step)


FC = 256


def mlp_kernel(parts, n_ref, x_ref, co_ref, cg_ref, o_ref, vec_ref, *rest):
    pieces = rest[:parts]
    out_ref, dh_ref, do_ref, send_ref, keep_ref, vb_ref, w, acc, vg, gbu, cpool, opool, bu_s, c_s, dy_s, ct_s, dyt_s, zb, db, ub, eb, out_s, dc_s, sems = rest[parts:]

    @pl.when(pl.program_id(0) == 0)
    def _():
        fetch(n_ref, pieces, w, sems)
        acc[...] = jnp.zeros_like(acc)
        vg[...] = jnp.zeros_like(vg)
        gbu[...] = jnp.zeros_like(gbu)
        fill_pool(co_ref, cg_ref, cpool)
        bu_s[...] = jnp.concatenate([vec_ref[8 + j : 9 + j] for j in range(F // D)], axis=1)

    def step():
        g2, b2, bo, bd = vec_ref[1:2], vec_ref[6:7], vec_ref[5:6], vec_ref[7:8]
        x = x_ref[0].astype(f32)
        o = o_ref[0]
        h = x + dot(o, w[:, :D]) + bo
        n2, r2 = norm(h)
        c = (n2 * g2 + b2).astype(bf16)
        dyf = load_image(n_ref, cpool)
        dy = dyf.astype(bf16)
        steps = F // FC
        c_s[...] = c
        dy_s[...] = dy
        ct_s[...] = c.T
        dyt_s[...] = dy.T

        def cols(base, j):
            return slice(base + j * FC, base + j * FC + FC)

        def produce(j, slot):
            zb[slot] = dot(c_s[...], w[:, cols(D, j)])
            db[slot] = dot(dy_s[...], w[:, cols(D + F, j)])

        def middle(j, slot):
            u, slope = gelu_parts(zb[slot] + bu_s[:, cols(0, j)])
            dz = db[slot] * slope
            gbu[:, cols(0, j)] += col8(dz)
            ub[slot] = u.astype(bf16)
            eb[slot] = dz.astype(bf16)

        def consume(j, slot, first=False):
            u, dzb = ub[slot], eb[slot]
            o1, d1 = dot_nt(u, w[:, cols(D + F, j)]), dot_nt(dzb, w[:, cols(D, j)])
            out_s[...] = o1 if first else out_s[...] + o1
            dc_s[...] = d1 if first else dc_s[...] + d1
            base = M_HALF * (j // (steps // 2)) + 256
            acc[:, cols(base, j % (steps // 2))] += dot(ct_s[...], dzb)
            acc[:, cols(base + F2, j % (steps // 2))] += dot(dyt_s[...], u)

        produce(0, 0)
        produce(1, 1)
        middle(0, 0)
        for j in range(1, steps):
            if j + 1 < steps:
                produce(j + 1, (j + 1) % 3)
            consume(j - 1, (j - 1) % 3, j == 1)
            middle(j, j % 3)
        consume(steps - 1, (steps - 1) % 3)
        out, dc = out_s[...], dc_s[...]
        store_image(n_ref, opool, h + out + bd)
        dh = dyf + norm_back(dc * g2, n2, r2)
        dh_ref[0] = dh
        dhb = dh.astype(bf16)
        ot = o.T
        acc[:, :256] += dot(ot, dhb[:, :256])
        acc[:, M_HALF : M_HALF + 128] += dot(ot, dhb[:, 256:])
        do_ref[0] = dot_nt(dhb, w[:, :D]).astype(bf16)
        vg[0:8] += col8(dc * n2)
        vg[8:16] += col8(dh)
        vg[16:24] += col8(dc)
        vg[24:32] += col8(dyf)

    live_step(n_ref, step)

    @pl.when(pl.program_id(0) == n_ref[0] - 1)
    def _():
        empty_pool(opool, out_ref)
        flush(n_ref, acc, send_ref, keep_ref)
        rows = [total(vg[8 * k : 8 * k + 8]) for k in range(4)]
        rows += [total(gbu[:, k * D : (k + 1) * D]) for k in range(F // D)]
        vb_ref[...] = jnp.concatenate(rows, axis=0)


def attn_bwd_kernel(parts, n_ref, x_ref, qkv_ref, lse_ref, do_ref, dh_ref, vec_ref, vb_ref, *rest):
    pieces = rest[:parts]
    out_ref, send_ref, keep_ref, w, acc, vg, dqkv, opool, sb, db, pb, gb, tb, sems = rest[parts:]

    @pl.when(pl.program_id(0) == 0)
    def _():
        fetch(n_ref, pieces, w, sems)
        acc[...] = jnp.zeros_like(acc)
        vg[...] = jnp.zeros_like(vg)

    def step():
        g1, b1 = vec_ref[0:1], vec_ref[2:3]
        x = x_ref[0].astype(f32)
        n1, r1 = norm(x)
        at_ = (n1 * g1 + b1).astype(bf16).T
        low = lax.broadcasted_iota(jnp.int32, (TP, 128), 1) < HD
        real = lax.broadcasted_iota(jnp.int32, (TP - TC, 128), 0) < T - TC

        def mask(h, v):
            return jnp.where(low if h % 2 == 0 else jnp.logical_not(low), v, jnp.zeros_like(v))

        def lanes(h, off=0):
            return slice(off + (h // 2) * 128, off + (h // 2) * 128 + 128)

        def produce(h):
            sb[h % 3] = dot_nt(mask(h, qkv_ref[0, :, lanes(h)]), qkv_ref[0, :, lanes(h, D)])
            db[h % 3] = dot_nt(mask(h, do_ref[0, :, lanes(h)]), qkv_ref[0, :, lanes(h, 2 * D)])

        def middle(h):
            p = jnp.exp2(sb[h % 3] * SCALE_LOG2E - lse_ref[0, :, h : h + 1])
            dp = db[h % 3]
            pb[h % 2] = p.astype(bf16)
            delta = jnp.sum(p * dp, axis=-1, keepdims=True)
            gb[h % 2] = (p * (dp - delta) * SCALE).astype(bf16)

        def consume(h):
            ds = gb[h % 2]
            part = (dot(ds, mask(h, qkv_ref[0, :, lanes(h, D)])),
                    dot_tn(ds, mask(h, qkv_ref[0, :, lanes(h)])),
                    dot_tn(pb[h % 2], mask(h, do_ref[0, :, lanes(h)])))
            if h % 2 == 0:
                for k in range(3):
                    tb[k] = part[k]
                return
            dq, dk, dv = (tb[k] + part[k] for k in range(3))
            dqkv[:, lanes(h)] = dq.astype(bf16)
            for v, off in ((dk, D), (dv, 2 * D)):
                v_b = v.astype(bf16)
                dqkv[:TC, lanes(h, off)] = v_b[:TC]
                dqkv[TC:, lanes(h, off)] = jnp.where(real, v_b[TC:], jnp.zeros_like(v_b[TC:]))
            vg[16:24, lanes(h)] += col8(dq)
            vg[24:32, lanes(h)] += col8(dv[:TC]) + col8(jnp.where(real, dv[TC:], 0.0))

        produce(0)
        produce(1)
        middle(0)
        for h in range(1, H):
            if h + 1 < H:
                produce(h + 1)
            consume(h - 1)
            middle(h)
        consume(H - 1)
        dqkv_b = dqkv[...]
        acc[:, : 3 * D] += dot(at_, dqkv_b)
        da = dot_nt(dqkv_b, w[:, : 3 * D])
        store_image(n_ref, opool, dh_ref[0] + norm_back(da * g1, n1, r1))
        vg[0:8] += col8(da * n1)
        vg[8:16] += col8(da)

    live_step(n_ref, step)

    @pl.when(pl.program_id(0) == n_ref[0] - 1)
    def _():
        empty_pool(opool, out_ref)
        mine = [total(vg[8 * k : 8 * k + 8]) for k in range(4)]
        vb = vb_ref[...]
        rows = jnp.concatenate([mine[0], vb[0:1], mine[1], mine[2], mine[3], vb[1:8], jnp.zeros((116, D), f32)], axis=0)
        acc[:, 3 * D :] = rows.T
        flush(n_ref, acc, send_ref, keep_ref)


def whole(shape):
    return pl.BlockSpec(shape, lambda i, n: (0,) * len(shape))


def item(rows, cols):
    return pl.BlockSpec((1, rows, cols), lambda i, n: (jnp.minimum(i, n[0] - 1), 0, 0))


def layer_call(kernel, n, slots, ins, in_specs, pieces, outs, out_specs, scratch, flops):
    parts = len(pieces)
    return pl.pallas_call(
        lambda *refs: kernel(parts, *refs),
        out_shape=outs,
        grid_spec=pltpu.PrefetchScalarGridSpec(
            num_scalar_prefetch=1, grid=(slots,), in_specs=list(in_specs) + [ANY] * parts,
            out_specs=out_specs, scratch_shapes=list(scratch) + [pltpu.SemaphoreType.DMA((parts,))]),
        compiler_params=pltpu.CompilerParams(
            dimension_semantics=("arbitrary",), vmem_limit_bytes=VMEM_LIMIT),
        cost_estimate=pl.CostEstimate(flops=flops, bytes_accessed=20_000_000, transcendentals=0))(n, *ins, *pieces)


def once(shape):
    return pl.BlockSpec(shape, lambda i, n: (0,) * len(shape), pipeline_mode=pl.Buffered(1))


def attn_fwd(n, slots, x_own, x_got, pieces):
    rows = x_own.shape[0]
    return layer_call(
        attn_fwd_kernel, n, slots, (x_own, x_got), (once((rows, D)), once((rows, D))), pieces,
        (S((slots, TP, D), bf16), S((slots, TP, 3 * D), bf16), S((slots, TP, D), bf16), S((slots, TP, 128), f32),
         S((16, D), f32)),
        (item(TP, D), item(TP, 3 * D), item(TP, D), item(TP, 128), whole((16, D))),
        (pltpu.VMEM((D, Q_COLS), bf16), pltpu.VMEM((D // 128, TP * slots, 128), f32)), 10_000_000_000)


def reduced(parts, cols):
    shape = (parts // 2, D // parts, cols)
    return (S(shape, bf16), S(shape, f32)), (once(shape), once(shape))


def mlp(n, slots, x, c_own, c_got, o, vec, pieces):
    rows = c_own.shape[0]
    r_shape, r_spec = reduced(len(pieces), 2 * M_HALF)
    return layer_call(
        mlp_kernel, n, slots, (x, c_own, c_got, o, vec),
        (item(TP, D), once((rows, D)), once((rows, D)), item(TP, D), whole((16, D))), pieces,
        (S((rows, D), bf16), S((slots, TP, D), f32), S((slots, TP, D), bf16)) + r_shape + (S((8, D), f32),),
        (once((rows, D)), item(TP, D), item(TP, D)) + r_spec + (whole((8, D)),),
        (pltpu.VMEM((D, R_COLS), bf16), pltpu.VMEM((D, 2 * M_HALF), f32), pltpu.VMEM((32, D), f32),
         pltpu.VMEM((8, F), f32), pltpu.VMEM((D // 128, TP * slots, 128), f32), pltpu.VMEM((D // 128, TP * slots, 128), f32),
         pltpu.VMEM((1, F), f32), pltpu.VMEM((TP, D), bf16), pltpu.VMEM((TP, D), bf16), pltpu.VMEM((D, TP), bf16),
         pltpu.VMEM((D, TP), bf16), pltpu.VMEM((3, TP, FC), f32), pltpu.VMEM((3, TP, FC), f32),
         pltpu.VMEM((3, TP, FC), bf16), pltpu.VMEM((3, TP, FC), bf16), pltpu.VMEM((TP, D), f32),
         pltpu.VMEM((TP, D), f32)),
        25_000_000_000)


def attn_bwd(n, slots, x, qkv, lse, do, dh, vec, vb, pieces, rows):
    r_shape, r_spec = reduced(len(pieces), Q_COLS)
    return layer_call(
        attn_bwd_kernel, n, slots, (x, qkv, lse, do, dh, vec, vb),
        (item(TP, D), item(TP, 3 * D), item(TP, 128), item(TP, D), item(TP, D),
         whole((16, D)), whole((8, D))), pieces,
        (S((rows, D), bf16),) + r_shape, (once((rows, D)),) + r_spec,
        (pltpu.VMEM((D, Q_COLS), bf16), pltpu.VMEM((D, Q_COLS), f32), pltpu.VMEM((32, D), f32),
         pltpu.VMEM((TP, 3 * D), bf16), pltpu.VMEM((D // 128, TP * slots, 128), f32), pltpu.VMEM((3, TP, TP), f32),
         pltpu.VMEM((3, TP, TP), f32), pltpu.VMEM((2, TP, TP), bf16), pltpu.VMEM((2, TP, TP), bf16),
         pltpu.VMEM((3, TP, 128), f32)), 20_000_000_000)


def pack_first_kernel(w_ref, g_ref, b_ref, o_ref):
    rows = w_ref.shape[0]
    vec = jnp.concatenate([g_ref[...], b_ref[...], jnp.zeros((128 - NV, rows), f32)], axis=0)
    o_ref[:, : 3 * D] = w_ref[...].astype(bf16)
    o_ref[:, 3 * D :] = vec.T.astype(bf16)


def pack_rest_kernel(p_ref, a_ref, b_ref, o_ref):
    o_ref[:, :D] = p_ref[...].astype(bf16)
    o_ref[:, D : D + F] = a_ref[...].astype(bf16)
    o_ref[:, D + F : D + 2 * F] = b_ref[...].astype(bf16)


def split3(a):
    hi = a.astype(bf16)
    return hi, (a - hi.astype(f32)).astype(bf16)


def dot3(a, b):
    return dot(jnp.concatenate([a[0], a[1], a[0]], axis=1), jnp.concatenate([b[0], b[0], b[1]], axis=0))


def orth_rows(m, q_s, at, rows):
    a = dot_nt(m, m)
    diag = lax.broadcasted_iota(jnp.int32, (D, D), 0) == lax.broadcasted_iota(jnp.int32, (D, D), 1)
    ssq = jnp.sum(jnp.where(diag, a, 0.0), axis=(0, 1), keepdims=True)
    s = 1.0 / (jnp.sqrt(ssq) + ORTHO_EPSILON)
    a = a * (s * s)
    eye = jnp.where(diag, COEFF_FIRST, 0.0)
    q = None
    for k in range(NS_ITERS - 1):
        a_s = split3(a)
        p = eye + COEFF_SECOND * a + COEFF_THIRD * dot3(a_s, a_s)
        p_s = split3(p)
        if k == 0:
            q_s[...] = p
            q = q_s[pl.ds(at, rows), :]
        else:
            q = dot3(split3(q), p_s)
        if k < NS_ITERS - 2:
            a = dot3(split3(dot3(p_s, a_s)), p_s)

    def times_last(v):
        return dot3(split3(dot3(split3(dot3(split3(v), p_s)), a_s)), p_s)

    qa = times_last(q)
    q = COEFF_FIRST * q + COEFF_SECOND * qa + COEFF_THIRD * times_last(qa)
    hi, lo = split3(q * s)
    return dot(hi, m) + dot(lo, m)


def fetch_momenta(n_ref, pieces, buf, sems, plan):
    rows = pieces[0].shape[1]

    def start(x):
        copies = []
        for k in range(2):
            own, near, far = pieces[3 * k : 3 * k + 3]
            for off, src, h in ((0, own.at[0], 0), (0, own.at[1], 1), (2, near, x), (2, far, 1 - x)):
                col, width, to = plan(h)
                at = pl.multiple_of((n_ref[0] ^ (k + off)) * rows, 32)
                copies.append(pltpu.make_async_copy(
                    src.at[:, pl.ds(col, width)], buf.at[pl.ds(at, rows), pl.ds(to, width)], sems.at[len(copies)]))
        for c in copies:
            c.start()
        for c in copies:
            c.wait()

    for x in range(2):
        pl.when(n_ref[1] == x)(lambda x=x: start(x))


def orth_both(n_ref, mine_ref, theirs_ref, m, q_s, o_s):
    rows = mine_ref.shape[0]
    core = n_ref[0] & 1
    at = pl.multiple_of((n_ref[0] - core) * rows, 32)
    o_s[...] = orth_rows(m[...], q_s, at, 2 * rows)
    mine_ref[...] = o_s[pl.ds(pl.multiple_of(core * rows, 32), rows), :]
    theirs_ref[...] = o_s[pl.ds(pl.multiple_of((1 - core) * rows, 32), rows), :]


def orth_mlp_kernel(n_ref, *rest):
    pieces = rest[:6]
    mine_ref, theirs_ref, m, q_s, o_s, sems = rest[6:]
    at = pl.multiple_of(256 + (n_ref[0] & 1) * F2, 128)
    fetch_momenta(n_ref, pieces, m, sems, lambda h: (at, F2, h * F2))
    orth_both(n_ref, mine_ref, theirs_ref, m, q_s, o_s)


def orth_attn_kernel(n_ref, *rest):
    pieces, others = rest[:6], rest[6:12]
    mine_ref, theirs_ref, m, q_s, o_s, sems = rest[12:]

    @pl.when(n_ref[0] & 1 == 0)
    def _():
        fetch_momenta(n_ref, pieces, m, sems, lambda h: (0, 3 * D - Q_HALF if h else Q_HALF, h * Q_HALF))

    @pl.when(n_ref[0] & 1 == 1)
    def _():
        m[:, D:] = jnp.zeros((D, 2 * D), bf16)
        fetch_momenta(n_ref, others, m, sems, lambda h: (0, D - 256 if h else 256, h * 256))

    orth_both(n_ref, mine_ref, theirs_ref, m, q_s, o_s)


def orth_call(kernel, at, pieces, cols):
    rows = pieces[0].shape[1]
    spec = pl.BlockSpec((rows, cols), lambda i, n: (0, 0))
    return pl.pallas_call(
        kernel, out_shape=(S((rows, cols), f32),) * 2,
        grid_spec=pltpu.PrefetchScalarGridSpec(
            num_scalar_prefetch=1, grid=(1,), in_specs=[ANY] * len(pieces), out_specs=(spec,) * 2,
            scratch_shapes=[pltpu.VMEM((D, cols), bf16), pltpu.VMEM((D, D), f32), pltpu.VMEM((2 * rows, cols), f32),
                            pltpu.SemaphoreType.DMA((8,))]),
        compiler_params=pltpu.CompilerParams(vmem_limit_bytes=VMEM_LIMIT),
        cost_estimate=pl.CostEstimate(flops=8_000_000_000, bytes_accessed=4_000_000, transcendentals=0))(at, *pieces)


def step_call(kernel, at, ins, outs, scratch):
    full = [pl.BlockSpec(v.shape, lambda i, n, r=len(v.shape): (0,) * r) for v in ins]
    return pl.pallas_call(
        kernel, out_shape=outs,
        grid_spec=pltpu.PrefetchScalarGridSpec(
            num_scalar_prefetch=1, grid=(1,), in_specs=full,
            out_specs=tuple(pl.BlockSpec(v.shape, lambda i, n, r=len(v.shape): (0,) * r) for v in outs),
            scratch_shapes=scratch),
        compiler_params=pltpu.CompilerParams(vmem_limit_bytes=VMEM_LIMIT),
        cost_estimate=pl.CostEstimate(flops=1_000_000, bytes_accessed=1_000_000, transcendentals=0))(at, *ins)


def split_xy_kernel(n_ref, keep_ref, got_ref, own_ref, x_ref, y_ref, xy_ref):
    half = own_ref.shape[1]

    def term(dy, dx):
        y, at = n_ref[0] >> 1 ^ dy, pl.multiple_of((n_ref[1] ^ dx) * half, 128)
        return keep_ref[y, :, pl.ds(at, half)] + got_ref[y, :, pl.ds(at, half)].astype(f32)

    own_ref[...] = term(0, 0)
    x_ref[...] = term(0, 1).astype(bf16)
    y_ref[...] = term(1, 0).astype(bf16)
    xy_ref[...] = term(1, 1).astype(bf16)


def split_z_kernel(n_ref, own_ref, a_ref, b_ref, c_ref, keep_ref, *rest):
    sends, t = rest[:3], rest[3]
    t[...] = own_ref[...] + (a_ref[...].astype(f32) + b_ref[...].astype(f32) + c_ref[...].astype(f32))
    rows = keep_ref.shape[0]
    keep_ref[...] = t[pl.ds(pl.multiple_of(n_ref[2] * rows, 8), rows), :]
    for k, ref in enumerate(sends):
        ref[...] = t[pl.ds(pl.multiple_of((n_ref[2] ^ (k + 1)) * rows, 8), rows), :].astype(bf16)


def sum_z_kernel(n_ref, own_ref, a_ref, b_ref, c_ref, o_ref):
    t = own_ref[...] + (a_ref[...].astype(f32) + b_ref[...].astype(f32) + c_ref[...].astype(f32))
    o_ref[...] = t.astype(o_ref.dtype)


def momentum(g, mom, scale):
    return MUON_MOMENTUM * mom + g.astype(f32) * scale


def momenta_kernel(scale, plan, n_ref, own_ref, a_ref, b_ref, c_ref, *rest):
    moms, (g_ref, m_ref) = rest[:-2], rest[-2:]
    rows = own_ref.shape[0]
    for k, ref in enumerate((own_ref, a_ref, b_ref, c_ref)):
        g_ref[pl.ds(pl.multiple_of((n_ref[2] ^ k) * rows, 8), rows), :] = ref[...]
    m_ref[...] = jnp.zeros_like(m_ref)

    def fill(h):
        for which, col, width, at in plan(h):
            m_ref[:, at : at + width] = momentum(
                g_ref[:, at : at + width], moms[which][:, col : col + width], scale).astype(bf16)

    for h in range(2):
        pl.when(n_ref[1] == h)(lambda h=h: fill(h))


def results_kernel(scale, plan, count, n_ref, own_ref, got_ref, *rest):
    moms, grads, nexts, m_ref = rest[:count], rest[count : 2 * count], rest[2 * count : 3 * count], rest[3 * count]
    m_ref[...] = jnp.zeros_like(m_ref)

    def fill(x):
        for h in range(2):
            src = own_ref if h == x else got_ref
            for which, col, width, at in plan(h):
                g = src[:, at : at + width]
                m = momentum(g, moms[which][:, col : col + width], scale)
                grads[which][:, col : col + width] = g.astype(f32) * scale
                nexts[which][:, col : col + width] = m
                m_ref[h, :, at : at + width] = m.astype(bf16)

    for x in range(2):
        pl.when(n_ref[1] == x)(lambda x=x: fill(x))


def mlp_plan(h):
    return ((0, 256 * h, D - 256 if h else 256, 0), (1, F2 * h, F2, 256), (2, F2 * h, F2, 256 + F2))


def attn_plan(h):
    return ((0, Q_HALF * h, 3 * D - Q_HALF if h else Q_HALF, 0),)


def send(v, rep, fsdp):
    parts = lax.axis_size("fsdp")
    pairs = [(r * parts + f, (r ^ rep) * parts + (f ^ fsdp)) for r in range(lax.axis_size("rep")) for f in range(parts)]
    return lax.ppermute(v, ("rep", "fsdp"), pairs)


def spread_xy(at, sent, keep):
    got = send(sent, 0, 1)
    half = S((keep.shape[1], keep.shape[2] // 2), bf16)
    own, to_x, to_y, to_xy = step_call(
        split_xy_kernel, at, (keep, got), (S(half.shape, f32), half, half, half), [])
    return own, send(to_x, 1, 0), send(to_y, 0, 2), send(to_xy, 1, 2)


def sum_all(at, terms, moms, plan, scale):
    rows, half = terms[0].shape
    z = S((rows // 4, half), bf16)
    out = step_call(split_z_kernel, at, terms, (S(z.shape, f32), z, z, z), [pltpu.VMEM((rows, half), f32)])
    got = [send(v, 2 * (k + 1), 0) for k, v in enumerate(out[1:])]
    more = range(3, lax.axis_size("rep").bit_length() - 1)
    (g,) = step_call(sum_z_kernel, at, (out[0], *got), (S(z.shape, f32 if more else bf16),), [])
    for b in more:
        g = g.astype(bf16).astype(f32) + send(g.astype(bf16), 1 << b, 0).astype(f32)
    g = g.astype(bf16)
    got = [send(g, 2 * k, 0) for k in range(1, 4)]
    both = S((rows, half), bf16)
    g, m = step_call(lambda *refs: momenta_kernel(scale, plan, *refs), at, (g, *got, *moms), (both, both), [])
    near, far, g_x = send(m, 0, 2), send(m, 1, 2), send(g, 1, 0)
    count = len(moms)
    full = tuple(S(v.shape, f32) for v in moms)
    out = step_call(lambda *refs: results_kernel(scale, plan, count, *refs), at, (g, g_x, *moms),
                    full + full + (S((2, rows, half), bf16),), [])
    own = out[-1]
    pieces = [own, near, far] + [send(v, 0, 1) for v in (own, near, far)]
    return g, g_x, out[:count], out[count : 2 * count], pieces


def swap(v, axis, k):
    return lax.ppermute(v, axis, [(i, i ^ k) for i in range(lax.axis_size(axis))])


def bits(axis):
    return range(lax.axis_size(axis).bit_length() - 1)


def all_pieces(v, axis):
    pieces = {0: v}
    for b in reversed(bits(axis)):
        pieces.update({k ^ (1 << b): swap(p, axis, 1 << b) for k, p in list(pieces.items())})
    return [pieces[k] for k in range(lax.axis_size(axis))]


def unpool_kernel(slots, n_ref, own_ref, got_ref, o_ref):
    row = pl.program_id(0) * own_ref.shape[0] + lax.broadcasted_iota(jnp.int32, own_ref.shape, 0)
    slot = row & (slots - 1)
    v = jnp.where(slot & 1 == 0, own_ref[...].astype(f32), got_ref[...].astype(f32))
    o_ref[...] = jnp.where(slot < n_ref[0], v, 0.0).astype(bf16)


def unpool_call(count, slots, own, got):
    rows = own.shape[0]
    block = rows // 2 if rows % 16 == 0 else rows
    spec = pl.BlockSpec((block, D), lambda i, n: (i, 0))
    return pl.pallas_call(
        lambda *refs: unpool_kernel(slots, *refs), out_shape=S(own.shape, bf16),
        grid_spec=pltpu.PrefetchScalarGridSpec(
            num_scalar_prefetch=1, grid=(rows // block,), in_specs=[spec, spec], out_specs=spec),
        cost_estimate=pl.CostEstimate(flops=1_000_000, bytes_accessed=7_000_000, transcendentals=0))(count, own, got)


def adam_kernel(scale, n_ref, own_ref, got_ref, *refs):
    ins, outs = refs[:6], refs[6:]
    g = jnp.where(n_ref[1] == 1, own_ref[...], got_ref[...])
    g = (g.astype(f32) * scale).T
    for k, (lo, hi) in enumerate(((0, 2), (2, NV))):
        gradient, parameter = g[lo:hi], ins[k][...]
        first = ADAM_FIRST * ins[2 + 2 * k][...] + (1.0 - ADAM_FIRST) * gradient
        second = ADAM_SECOND * ins[3 + 2 * k][...] + (1.0 - ADAM_SECOND) * gradient * gradient
        first_hat = first / (1.0 - ADAM_FIRST**ADAM_STEP)
        second_hat = second / (1.0 - ADAM_SECOND**ADAM_STEP)
        outs[k][...] = gradient
        outs[2 + k][...] = parameter - ADAM_RATE * (
            first_hat / (jnp.sqrt(second_hat) + ADAM_EPSILON) + ADAM_DECAY * parameter)
        outs[4 + 2 * k][...] = first
        outs[5 + 2 * k][...] = second


def adam(at, own, got, devices, *states):
    full = [pl.BlockSpec(v.shape, lambda i, n: (0, 0)) for v in states]
    one, two = S(states[0].shape, f32), S(states[1].shape, f32)
    last = pl.BlockSpec((own.shape[0], 128), lambda i, n: (0, Q_HALF // 128 - 1))
    return pl.pallas_call(
        lambda *refs: adam_kernel(1.0 / devices, *refs),
        out_shape=(one, two, one, two, one, one, two, two),
        grid_spec=pltpu.PrefetchScalarGridSpec(
            num_scalar_prefetch=1, grid=(1,), in_specs=[last, last] + full,
            out_specs=tuple(full[k] for k in (0, 1, 0, 1, 2, 3, 4, 5))), name="adam")(at, own, got, *states)


def muon_factor(row_total, column_total):
    return math.sqrt(max(1.0, row_total / column_total))


def body(images, cotangent, counts, w_qkv, w_proj, w_fc1, w_fc2, gains, biases,
         mom_qkv, mom_proj, mom_fc1, mom_fc2, gains_first, gains_second, biases_first, biases_second):
    slots = images.shape[0]
    rows = w_qkv.shape[0]
    devices = lax.axis_size("rep") * lax.axis_size("fsdp")
    me = lax.axis_index("fsdp").astype(jnp.int32)

    first = pl.pallas_call(pack_first_kernel, out_shape=S((rows, Q_COLS), bf16), name="pack_first")(w_qkv, gains, biases)
    q_pieces = all_pieces(first, "fsdp")

    count = counts[0]
    other = swap(counts, "fsdp", 1)[0]
    x_own = images.transpose(1, 0, 2).reshape(-1, D)
    x_got = swap(x_own, "fsdp", 1)
    c_own = cotangent.transpose(1, 0, 2).reshape(-1, D)
    c_got = swap(c_own, "fsdp", 1)
    n_own, n_got = (count + 1) >> 1, other >> 1
    n = jnp.stack([n_own + n_got, n_own, me]).astype(jnp.int32)

    def unpool(v):
        full = unpool_call(count.reshape(1), slots, v, swap(v, "fsdp", 1))
        return full.reshape(-1, slots, D).transpose(1, 0, 2)

    rest = pl.pallas_call(pack_rest_kernel, out_shape=S((rows, R_COLS), bf16), name="pack_rest")(w_proj, w_fc1, w_fc2.T)
    r_pieces = all_pieces(rest, "fsdp")

    rep_at = lax.axis_index("rep").astype(jnp.int32)
    at = jnp.stack([me, rep_at & 1, (rep_at >> 1) & 3])
    x, qkv, o, lse, vec = attn_fwd(n, slots, x_own, x_got, q_pieces)
    out, dh, do, r_send, r_keep, vb = mlp(n, slots, x, c_own, c_got, o, vec, r_pieces)
    terms = spread_xy(at, r_send, r_keep)
    in_grad, q_send, q_keep = attn_bwd(n, slots, x, qkv, lse, do, dh, vec, vb, q_pieces, x_own.shape[0])
    scale = 1.0 / devices
    _, _, mid_grads, mid_nexts, mid_pieces = sum_all(
        at, terms, (mom_proj, mom_fc1, mom_fc2.T), mlp_plan, scale)
    g, g_x, (grad_qkv,), (next_qkv,), qkv_pieces = sum_all(
        at, spread_xy(at, q_send, q_keep), (mom_qkv,), attn_plan, scale)
    block_out = unpool(out)
    input_grad = unpool(in_grad)
    vectors = adam(at, g, g_x, devices, gains, biases, gains_first, gains_second, biases_first, biases_second)
    grad_proj, grad_fc1, grad_fc2t = mid_grads
    next_proj, next_fc1, next_fc2t = mid_nexts

    core = me & 1
    mine, theirs = orth_call(orth_mlp_kernel, at, mid_pieces, F)
    got = send(theirs, 0, 1)
    orth_fc1, orth_fc2t = jnp.where(core == 0, mine, got), jnp.where(core == 0, got, mine)
    mine, theirs = orth_call(orth_attn_kernel, at, qkv_pieces + mid_pieces, 3 * D)
    got = send(theirs, 0, 1)
    orth_qkv, orth_proj = jnp.where(core == 0, mine, got), jnp.where(core == 0, got, mine)[:, :D]
    new_qkv = w_qkv - MUON_RATE * muon_factor(D, 3 * D) * orth_qkv
    new_proj = w_proj - MUON_RATE * muon_factor(D, D) * orth_proj
    new_fc1 = w_fc1 - MUON_RATE * muon_factor(D, F) * orth_fc1
    new_fc2t = w_fc2.T - MUON_RATE * muon_factor(F, D) * orth_fc2t
    grad_gains, grad_biases, new_gains, new_biases = vectors[:4]
    return (block_out, input_grad, grad_qkv, grad_proj, grad_fc1, grad_fc2t.T, grad_gains, grad_biases,
            new_qkv, new_proj, new_fc1, new_fc2t.T, new_gains, new_biases,
            next_qkv, next_proj, next_fc1, next_fc2t.T) + tuple(vectors[4:])


def solution(mesh):
    in_specs = (
        P(("rep", "fsdp"), None, None),
        P(("rep", "fsdp"), None, None),
        P(("rep", "fsdp")),
        P("fsdp", None),
        P("fsdp", None),
        P("fsdp", None),
        P(None, "fsdp"),
        P(None, "fsdp"),
        P(None, "fsdp"),
        P("fsdp", None),
        P("fsdp", None),
        P("fsdp", None),
        P(None, "fsdp"),
        P(None, "fsdp"),
        P(None, "fsdp"),
        P(None, "fsdp"),
        P(None, "fsdp"),
    )
    out_specs = (
        P(("rep", "fsdp"), None, None),
        P(("rep", "fsdp"), None, None),
        P("fsdp", None),
        P("fsdp", None),
        P("fsdp", None),
        P(None, "fsdp"),
        P(None, "fsdp"),
        P(None, "fsdp"),
        P("fsdp", None),
        P("fsdp", None),
        P("fsdp", None),
        P(None, "fsdp"),
        P(None, "fsdp"),
        P(None, "fsdp"),
        P("fsdp", None),
        P("fsdp", None),
        P("fsdp", None),
        P(None, "fsdp"),
        P(None, "fsdp"),
        P(None, "fsdp"),
        P(None, "fsdp"),
        P(None, "fsdp"),
    )
    return jax.shard_map(body, mesh=mesh, in_specs=in_specs, out_specs=out_specs, check_vma=False)
```

time: 876 us -> 338 us (0.39)
  matrix products: 387 us -> 0 us
  local copies, waits for them, and re-layouts: 156 us -> 8.49 us
  Pallas kernels: 0 us -> 121 us
  starting transfers between devices: 1.07 us -> 122 us
  waiting for transfers between devices: 180 us -> 79 us
  other arithmetic: 70.7 us -> 3.95 us
  blocking collectives: 56.2 us -> 0 us
  between operations: 19.3 us -> 2.24 us
    dot_general x78 -> x0, matrix products: 387 us -> none  [the longest x20 70.7 us: orthogonalize(): square = jnp.dot(current, current.T, precision=lax.Precision.HIGHEST)]
    ppermute x0 -> x45, starting transfers between devices: none -> 122 us  [the longest x34 118 us: send(): return lax.ppermute(v, ('rep', 'fsdp'), pairs)]
    pallas_call x0 -> x20, Pallas kernels: none -> 121 us  [the longest x3 49.6 us: layer_call(): pl.pallas_call(lambda *refs: kernel(parts, *refs), out_shape=outs, grid_s...]
    reduce_scatter x4 -> x0, waiting for transfers between devices: 81.5 us -> none  [the longest x1 35.8 us: body(): lax.psum_scatter(local_grads[3], 'fsdp', scatter_dimension=1, tiled=True)]
    ppermute x0 -> x45, waiting for transfers between devices: none -> 79 us  [the longest x34 60.4 us: send(): return lax.ppermute(v, ('rep', 'fsdp'), pairs)]
    psum x1 -> x0, waiting for transfers between devices: 72 us -> none  [body(): lax.psum((group_sums[0], group_sums[1], group_sums[2], group_sums[3], gro...]
    reshape x9 -> x0, local copies, waits for them, and re-layouts: 54.2 us -> none  [the longest x1 22.3 us: forward_pass(): projected = projected.reshape(slot_count, tokens, 3, H, HD)]
    convert_element_type x9 -> x0, local copies, waits for them, and re-layouts: 45.4 us -> none  [the longest x2 32.9 us: backward_pass(): qkv_grad_b = qkv_grad.astype(jnp.bfloat16)]
  transfers between devices with their start and end apart: 12 -> 45, of which waited for: 6 -> 17; matrix products, arithmetic and copies ran while one was open for 48% -> 1% of each run, Pallas kernels for 0% -> 25%
where the time goes in v1:
time: 338 us; the launch traced here: 337 us
  starting transfers between devices  122 us (36%)
  Pallas kernels  121 us (36%)
  waiting for transfers between devices  79 us (23%)
  local copies, waits for them, and re-layouts  8.49 us (3%)
  other arithmetic  3.95 us (1%)
    ppermute x34, starting transfers between devices, send(): return lax.ppermute(v, ('rep', 'fsdp'), pairs)  118 us
    ppermute x34, waiting for transfers between devices, send(): return lax.ppermute(v, ('rep', 'fsdp'), pairs)  60.4 us
    pallas_call x3, Pallas kernels, layer_call(): pl.pallas_call(lambda *refs: kernel(parts, *refs), out_shape=outs, grid_s...  49.6 us
    pallas_call x10, Pallas kernels, step_call(): pl.pallas_call(kernel, out_shape=outs, grid_spec=pltpu.PrefetchScalarGrid...  29.9 us
    pallas_call x2, Pallas kernels, orth_call(): pl.pallas_call(kernel, out_shape=(S((rows, cols), f32),) * 2, grid_spec=p...  27.4 us
    ppermute x11, waiting for transfers between devices, swap(): lax.ppermute(v, axis, [(i, i ^ k) for i in range(lax.axis_size(axis))])  18.7 us
    unnamed x76, local copies, waits for them, and re-layouts  8.49 us
    pallas_call x2, Pallas kernels, unpool_call(): pl.pallas_call(lambda *refs: unpool_kernel(slots, *refs), out_shape=S(own...  7.85 us
  transfers between devices with their start and end apart: 45, of which 17 were waited for; matrix products, arithmetic and copies ran while one was open for 1% of the time, Pallas kernels for 25%

profile of v1, /device:TPU:0, one launch (start us, length us, event | category | flops | bytes accessed | tf_op | source)
XLA Modules:
  0.0 337.1 jit_solution(12948376248249002673)
XLA Ops:
  9.8 17.2 %collective-permute-done.3.refs_5_.refs_10_ = bf16[96,1280]{1,0:T(8,128)(2,1)S(1)} collective-permute-done((bf16[96,1280]{1,0:T(8,128)(2,1)}, bf16[96,1280]{1,0:T(8,128)(2,1)S(1)}, u32[]{:S(2)}, u32[]{:S(2)}) %collective-permute-start.3) | collective-permute-done | bytes 245792 | tf_op jit(solution)/shard_map/ppermute | solution.py:675
  29.5 12.2 %shard_map.336 = (bf16[16,208,384]{2,1,0:T(8,128)(2,1)}, bf16[16,208,1152]{2,1,0:T(8,128)(2,1)}, bf16[16,208,384]{2,1,0:T(8,128)(2,1)}, f32[16,208,128]{2,1,0:T(8,128)}, f32[16,384]{1,0:T(8,128)}) custom-call(s32[3]{0:T(128)} %pad_add_fusion.refs_0_, bf16[3152,384]{1,0:T(8,128)(2,1)} %bitcast.28, bf16[3152,384]{1,0:T(8,128)(2,1)} %collective-permute-done.1.refs_2_, ...), custom_call_target="tpu_custom_call" | custom-call | flops 10000000000 | bytes 20000000 | tf_op jit(solution)/shard_map/pallas_call | solution.py:374
  43.2 21.8 %shard_map.337 = (bf16[3152,384]{1,0:T(8,128)(2,1)}, f32[16,208,384]{2,1,0:T(8,128)}, bf16[16,208,384]{2,1,0:T(8,128)(2,1)}, bf16[2,96,3584]{2,1,0:T(8,128)(2,1)...) custom-call(s32[3]{0:T(128)} %pad_add_fusion.refs_0_, bf16[16,208,384]{2,1,0:T(8,128)(2,1)} %get-tuple-element.78.refs_1_, ...), custom_call_target="tpu_custom_call" | custom-call | flops 24999999488 | bytes 20000000 | tf_op jit(solution)/shard_map/pallas_call | solution.py:374
  65.5 15.6 %shard_map.339 = (bf16[3152,384]{1,0:T(8,128)(2,1)}, bf16[2,96,1280]{2,1,0:T(8,128)(2,1)}, f32[2,96,1280]{2,1,0:T(8,128)}) custom-call(s32[3]{0:T(128)} %pad_add_fusion.refs_0_, bf16[16,208,384]{2,1,0:T(8,128)(2,1)} %get-tuple-element.78.refs_1_, bf16[16,208,1152]{2,1,0:T(8,128)(2,1)} %get-tuple-element.82.refs_2_, ...), custom_call_target="tpu_custom_call" | custom-call | flops 20000000000 | bytes 20000000 | tf_op jit(solution)/shard_map/pallas_call | solution.py:374
  82.4 4.2 %shard_map.346 = (f32[96,1792]{1,0:T(8,128)}, bf16[96,1792]{1,0:T(8,128)(2,1)}, bf16[96,1792]{1,0:T(8,128)(2,1)}, bf16[96,1792]{1,0:T(8,128)(2,1)}) custom-call(s32[3]{0:T(128)} %pad_add_fusion.1.n_ref.refs_0_, f32[2,96,3584]{2,1,0:T(8,128)} %get-tuple-element.100.keep_ref, bf16[2,96,3584]{2,1,0:T(8,128)(2,1)} %collective-permute-done.22.got_ref), custom_call_target="tpu_custom_call" | custom-call | flops 1000000 | bytes 1000000 | tf_op jit(solution)/shard_map/pallas_call | solution.py:554
  88.3 8.8 %collective-permute-start.24 = (bf16[96,1792]{1,0:T(8,128)(2,1)}, bf16[96,1792]{1,0:T(8,128)(2,1)S(1)}, u32[]{:S(2)}, u32[]{:S(2)}) collective-permute-start(bf16[96,1792]{1,0:T(8,128)(2,1)} %get-tuple-element.104), channel_id=1, source_target_pairs={{0,2},{1,3},{2,0},{3,1},{4,6},{5,7},{6,4},{7,5},{8,10},{9,11},{10,... | collective-permute-start | bytes 1032200 | tf_op jit(solution)/shard_map/ppermute | solution.py:640
  97.5 14.6 %collective-permute-done.24.b_ref = bf16[96,1792]{1,0:T(8,128)(2,1)S(1)} collective-permute-done((bf16[96,1792]{1,0:T(8,128)(2,1)}, bf16[96,1792]{1,0:T(8,128)(2,1)S(1)}, u32[]{:S(2)}, u32[]{:S(2)}) %collective-permute-start.24) | collective-permute-done | bytes 344096 | tf_op jit(solution)/shard_map/ppermute | solution.py:640
  116.9 40.1 %collective-permute-start.26 = (bf16[24,1792]{1,0:T(8,128)(2,1)}, bf16[24,1792]{1,0:T(8,128)(2,1)S(1)}, u32[]{:S(2)}, u32[]{:S(2)}) collective-permute-start(bf16[24,1792]{1,0:T(8,128)(2,1)} %get-tuple-element.107), channel_id=1, source_target_pairs={{0,8},{1,9},{2,10},{3,11},{4,12},{5,13},{6,14},{7,15},{8,0},{9,1},... | collective-permute-start | bytes 258056 | tf_op jit(solution)/shard_map/ppermute | solution.py:640
  157.0 41.1 %collective-permute-start.27 = (bf16[24,1792]{1,0:T(8,128)(2,1)}, bf16[24,1792]{1,0:T(8,128)(2,1)S(1)}, u32[]{:S(2)}, u32[]{:S(2)}) collective-permute-start(bf16[24,1792]{1,0:T(8,128)(2,1)} %get-tuple-element.108), channel_id=1, source_target_pairs={{0,16},{1,17},{2,18},{3,19},{4,20},{5,21},{6,22},{7,23},{8,24},{9,... | collective-permute-start | bytes 258056 | tf_op jit(solution)/shard_map/ppermute | solution.py:640
  198.1 4.5 %collective-permute-start.28 = (bf16[24,1792]{1,0:T(8,128)(2,1)}, bf16[24,1792]{1,0:T(8,128)(2,1)S(1)}, u32[]{:S(2)}, u32[]{:S(2)}) collective-permute-start(bf16[24,1792]{1,0:T(8,128)(2,1)} %get-tuple-element.109), channel_id=1, source_target_pairs={{0,24},{1,25},{2,26},{3,27},{4,28},{5,29},{6,30},{7,31},{8,16},{9,... | collective-permute-start | bytes 258056 | tf_op jit(solution)/shard_map/ppermute | solution.py:640
  208.5 3.7 %collective-permute-start.31 = (bf16[24,1792]{1,0:T(8,128)(2,1)}, bf16[24,1792]{1,0:T(8,128)(2,1)S(1)}, u32[]{:S(2)}, u32[]{:S(2)}) collective-permute-start(bf16[24,1792]{1,0:T(8,128)(2,1)} %shard_map.348.refs_1_), channel_id=1, source_target_pairs={{0,24},{1,25},{2,26},{3,27},{4,28},{5,29},{6,30},{7,31},{8,16},{9,... | collective-permute-start | bytes 258056 | tf_op jit(solution)/shard_map/ppermute | solution.py:640
  217.9 5.0 %collective-permute-done.30.refs_3_ = bf16[24,1792]{1,0:T(8,128)(2,1)S(1)} collective-permute-done((bf16[24,1792]{1,0:T(8,128)(2,1)}, bf16[24,1792]{1,0:T(8,128)(2,1)S(1)}, u32[]{:S(2)}, u32[]{:S(2)}) %collective-permute-start.30) | collective-permute-done | bytes 86048 | tf_op jit(solution)/shard_map/ppermute | solution.py:640
  225.0 3.1 shard_map.349
  239.2 5.1 %collective-permute-done.17.c_ref = bf16[24,640]{1,0:T(8,128)(2,1)S(1)} collective-permute-done((bf16[24,640]{1,0:T(8,128)(2,1)}, bf16[24,640]{1,0:T(8,128)(2,1)S(1)}, u32[]{:S(2)}, u32[]{:S(2)}) %collective-permute-start.17) | collective-permute-done | bytes 30752 | tf_op jit(solution)/shard_map/ppermute | solution.py:640
  248.2 4.7 %collective-permute-done.20.refs_4_ = bf16[24,640]{1,0:T(8,128)(2,1)S(1)} collective-permute-done((bf16[24,640]{1,0:T(8,128)(2,1)}, bf16[24,640]{1,0:T(8,128)(2,1)S(1)}, u32[]{:S(2)}, u32[]{:S(2)}) %collective-permute-start.20) | collective-permute-done | bytes 30752 | tf_op jit(solution)/shard_map/ppermute | solution.py:640
  253.6 3.4 %collective-permute-done.18.refs_2_ = bf16[24,640]{1,0:T(8,128)(2,1)S(1)} collective-permute-done((bf16[24,640]{1,0:T(8,128)(2,1)}, bf16[24,640]{1,0:T(8,128)(2,1)S(1)}, u32[]{:S(2)}, u32[]{:S(2)}) %collective-permute-start.18) | collective-permute-done | bytes 30752 | tf_op jit(solution)/shard_map/ppermute | solution.py:640
  262.9 3.3 collective-permute-done.34.rest_2_
  268.3 4.2 %shard_map.350 = (f32[96,384]{1,0:T(8,128)}, f32[96,1536]{1,0:T(8,128)}, f32[96,1536]{1,0:T(8,128)}, f32[96,384]{1,0:T(8,128)}, f32[96,1536]{1,0:T(8,128)}, /*in...) custom-call(s32[3]{0:T(128)} %pad_add_fusion.1.n_ref.refs_0_, bf16[96,1792]{1,0:T(8,128)(2,1)} %get-tuple-element.110.refs_1_, ...), custom_call_target="tpu_custom_call" | custom-call | flops 1000000 | bytes 1000000 | tf_op jit(solution)/shard_map/pallas_call | solution.py:554
  275.4 8.0 %collective-permute-done.39.rest_8_.rest_2_ = bf16[96,1792]{1,0:T(8,128)(2,1)} collective-permute-done((bf16[96,1792]{1,0:T(8,128)(2,1)S(1)}, bf16[96,1792]{1,0:T(8,128)(2,1)}, u32[]{:S(2)}, u32[]{:S(2)}) %collective-permute-start.39) | collective-permute-done | bytes 344096 | tf_op jit(solution)/shard_map/ppermute | solution.py:640
  283.4 7.3 %collective-permute-done.38.rest_7_.rest_1_ = bf16[96,1792]{1,0:T(8,128)(2,1)} collective-permute-done((bf16[96,1792]{1,0:T(8,128)(2,1)S(1)}, bf16[96,1792]{1,0:T(8,128)(2,1)}, u32[]{:S(2)}, u32[]{:S(2)}) %collective-permute-start.38) | collective-permute-done | bytes 344096 | tf_op jit(solution)/shard_map/ppermute | solution.py:640
  296.4 3.9 %shard_map.340 = bf16[3152,384]{1,0:T(8,128)(2,1)} custom-call(s32[1]{0:T(128)S(6)} %copy.39.refs_0_, bf16[3152,384]{1,0:T(8,128)(2,1)} %get-tuple-element.87.refs_1_, bf16[3152,384]{1,0:T(8,128)(2,1)} %collective-permute-done.10.refs_2_), custom_call_target="tpu_custom_call" | custom-call | flops 1000000 | bytes 7000000 | tf_op jit(solution)/shard_map/pallas_call | solution.py:700
  300.3 3.9 %shard_map.338 = bf16[3152,384]{1,0:T(8,128)(2,1)} custom-call(s32[1]{0:T(128)S(6)} %copy.39.refs_0_, bf16[3152,384]{1,0:T(8,128)(2,1)} %get-tuple-element.81.refs_1_, bf16[3152,384]{1,0:T(8,128)(2,1)} %collective-permute-done.9.refs_2_), custom_call_target="tpu_custom_call" | custom-call | flops 1000000 | bytes 7000000 | tf_op jit(solution)/shard_map/pallas_call | solution.py:700
  305.9 13.3 %shard_map.351 = (f32[96,1152]{1,0:T(8,128)}, f32[96,1152]{1,0:T(8,128)}) custom-call(s32[3]{0:T(128)} %pad_add_fusion.1.n_ref.refs_0_, bf16[2,96,640]{2,1,0:T(8,128)(2,1)} %get-tuple-element.116.rest_0_, bf16[96,640]{1,0:T(8,128)(2,1)} %copy-done.35, bf16[96,640]{1,0:T(8,128)(2,1)} %copy-done.34, bf16[2,96,640]{2,1,0:T(8,128)(2,1)} %collective-permute-done.35.rest_3_, ...), custom_call_target="tpu_custom_call" | custom-call | flops 8000000000 | bytes 4000000 | tf_op jit(solution)/shard_map/pallas_call | solution.py:542
  319.5 14.1 %shard_map.352 = (f32[96,1536]{1,0:T(8,128)}, f32[96,1536]{1,0:T(8,128)}) custom-call(s32[3]{0:T(128)} %pad_add_fusion.1.n_ref.refs_0_, bf16[2,96,1792]{2,1,0:T(8,128)(2,1)} %get-tuple-element.118.rest_6_.rest_0_, bf16[96,1792]{1,0:T(8,128)(2,1)} %collective-permute-done.38.rest_7_.rest_1_, bf16[96,1792]{1,0:T(8,128)(2,1)} %collective-permute-done.39.rest_8_.rest_2_, ...), custom_call_target="tpu_custom_call" | custom-call | flops 8000000000 | bytes 4000000 | tf_op jit(solution)/shard_map/pallas_call | solution.py:542
  (167 shorter events, 71.6 us)
Async XLA Ops:
  0.7 28.9 %collective-permute-start.1 = (bf16[3152,384]{1,0:T(8,128)(2,1)}, bf16[3152,384]{1,0:T(8,128)(2,1)}, u32[]{:S(2)}, u32[]{:S(2)}) collective-permute-start(bf16[3152,384]{1,0:T(8,128)(2,1)} %bitcast.27), channel_id=1, source_target_pairs={{0,1},{1,0},{2,3},{3,2},{4,5},{5,4},{6,7},{7,6},{8,9},{9,8},{10,11... | collective-permute-start | bytes 7262216 | tf_op jit(solution)/shard_map/ppermute | solution.py:675
  1.2 40.5 %collective-permute-start.5 = (bf16[3152,384]{1,0:T(8,128)(2,1)}, bf16[3152,384]{1,0:T(8,128)(2,1)S(1)}, u32[]{:S(2)}, u32[]{:S(2)}) collective-permute-start(bf16[3152,384]{1,0:T(8,128)(2,1)} %bitcast.29), channel_id=1, source_target_pairs={{0,1},{1,0},{2,3},{3,2},{4,5},{5,4},{6,7},{7,6},{8,9},{9,8},{10,11... | collective-permute-start | bytes 7262216 | tf_op jit(solution)/shard_map/ppermute | solution.py:675
  3.5 26.0 %collective-permute-start.7 = (bf16[96,3456]{1,0:T(8,128)(2,1)}, bf16[96,3456]{1,0:T(8,128)(2,1)S(1)}, u32[]{:S(2)}, u32[]{:S(2)}) collective-permute-start(bf16[96,3456]{1,0:T(8,128)(2,1)} %pack_rest.1.refs_6_), channel_id=1, source_target_pairs={{0,2},{1,3},{2,0},{3,1},{4,6},{5,7},{6,4},{7,5},{8,10},{9,11},{10,... | collective-permute-start | bytes 1990664 | tf_op jit(solution)/shard_map/ppermute | solution.py:675
  8.2 18.8 %collective-permute-start.3 = (bf16[96,1280]{1,0:T(8,128)(2,1)}, bf16[96,1280]{1,0:T(8,128)(2,1)S(1)}, u32[]{:S(2)}, u32[]{:S(2)}) collective-permute-start(bf16[96,1280]{1,0:T(8,128)(2,1)} %pack_first.1.refs_3_.refs_8_), channel_id=1, source_target_pairs={{0,2},{1,3},{2,0},{3,1},{4,6},{5,7},{6,4},{7,5},{8,10},{9,11},{10,... | collective-permute-start | bytes 737288 | tf_op jit(solution)/shard_map/ppermute | solution.py:675
  9.7 19.3 %collective-permute-start.2 = (bf16[96,1280]{1,0:T(8,128)(2,1)}, bf16[96,1280]{1,0:T(8,128)(2,1)}, u32[]{:S(2)}, u32[]{:S(2)}) collective-permute-start(bf16[96,1280]{1,0:T(8,128)(2,1)} %pack_first.1.refs_3_.refs_8_), channel_id=1, source_target_pairs={{0,1},{1,0},{2,3},{3,2},{4,5},{5,4},{6,7},{7,6},{8,9},{9,8},{10,11... | collective-permute-start | bytes 737288 | tf_op jit(solution)/shard_map/ppermute | solution.py:675
  28.9 12.8 %collective-permute-start.6 = (bf16[96,3456]{1,0:T(8,128)(2,1)}, bf16[96,3456]{1,0:T(8,128)(2,1)}, u32[]{:S(2)}, u32[]{:S(2)}) collective-permute-start(bf16[96,3456]{1,0:T(8,128)(2,1)} %pack_rest.1.refs_6_), channel_id=1, source_target_pairs={{0,1},{1,0},{2,3},{3,2},{4,5},{5,4},{6,7},{7,6},{8,9},{9,8},{10,11... | collective-permute-start | bytes 1990664 | tf_op jit(solution)/shard_map/ppermute | solution.py:675
  29.4 12.3 %collective-permute-start.8 = (bf16[96,3456]{1,0:T(8,128)(2,1)S(1)}, bf16[96,3456]{1,0:T(8,128)(2,1)}, u32[]{:S(2)}, u32[]{:S(2)}) collective-permute-start(bf16[96,3456]{1,0:T(8,128)(2,1)S(1)} %collective-permute-done.7.refs_8_), channel_id=1, source_target_pairs={{0,1},{1,0},{2,3},{3,2},{4,5},{5,4},{6,7},{7,6},{8,9},{9,8},{10,11... | collective-permute-start | bytes 1990664 | tf_op jit(solution)/shard_map/ppermute | solution.py:675
  65.0 17.4 %collective-permute-start.22 = (bf16[2,96,3584]{2,1,0:T(8,128)(2,1)}, bf16[2,96,3584]{2,1,0:T(8,128)(2,1)}, u32[]{:S(2)}, u32[]{:S(2)}) collective-permute-start(bf16[2,96,3584]{2,1,0:T(8,128)(2,1)} %get-tuple-element.101), channel_id=1, source_target_pairs={{0,1},{1,0},{2,3},{3,2},{4,5},{5,4},{6,7},{7,6},{8,9},{9,8},{10,11... | collective-permute-start | bytes 4128776 | tf_op jit(solution)/shard_map/ppermute | solution.py:640
  81.1 212.5 %collective-permute-start.10 = (bf16[3152,384]{1,0:T(8,128)(2,1)}, bf16[3152,384]{1,0:T(8,128)(2,1)}, u32[]{:S(2)}, u32[]{:S(2)}) collective-permute-start(bf16[3152,384]{1,0:T(8,128)(2,1)} %get-tuple-element.87.refs_1_), channel_id=1, source_target_pairs={{0,1},{1,0},{2,3},{3,2},{4,5},{5,4},{6,7},{7,6},{8,9},{9,8},{10,11... | collective-permute-start | bytes 7262216 | tf_op jit(solution)/shard_map/ppermute | solution.py:675
  81.3 212.8 %collective-permute-start.9 = (bf16[3152,384]{1,0:T(8,128)(2,1)S(1)}, bf16[3152,384]{1,0:T(8,128)(2,1)}, u32[]{:S(2)}, u32[]{:S(2)}) collective-permute-start(bf16[3152,384]{1,0:T(8,128)(2,1)S(1)} %copy-done), channel_id=1, source_target_pairs={{0,1},{1,0},{2,3},{3,2},{4,5},{5,4},{6,7},{7,6},{8,9},{9,8},{10,11... | collective-permute-start | bytes 7262216 | tf_op jit(solution)/shard_map/ppermute | solution.py:675
  88.3 23.8 %collective-permute-start.24 = (bf16[96,1792]{1,0:T(8,128)(2,1)}, bf16[96,1792]{1,0:T(8,128)(2,1)S(1)}, u32[]{:S(2)}, u32[]{:S(2)}) collective-permute-start(bf16[96,1792]{1,0:T(8,128)(2,1)} %get-tuple-element.104), channel_id=1, source_target_pairs={{0,2},{1,3},{2,0},{3,1},{4,6},{5,7},{6,4},{7,5},{8,10},{9,11},{10,... | collective-permute-start | bytes 1032200 | tf_op jit(solution)/shard_map/ppermute | solution.py:640
  97.1 16.0 %collective-permute-start.25 = (bf16[96,1792]{1,0:T(8,128)(2,1)}, bf16[96,1792]{1,0:T(8,128)(2,1)S(1)}, u32[]{:S(2)}, u32[]{:S(2)}) collective-permute-start(bf16[96,1792]{1,0:T(8,128)(2,1)} %get-tuple-element.105), channel_id=1, source_target_pairs={{0,6},{1,7},{2,4},{3,5},{4,2},{5,3},{6,0},{7,1},{8,14},{9,15},{10,... | collective-permute-start | bytes 1032200 | tf_op jit(solution)/shard_map/ppermute | solution.py:640
  97.5 114.7 %collective-permute-start.11 = (bf16[2,96,1280]{2,1,0:T(8,128)(2,1)}, bf16[2,96,1280]{2,1,0:T(8,128)(2,1)S(1)}, u32[]{:S(2)}, u32[]{:S(2)}) collective-permute-start(bf16[2,96,1280]{2,1,0:T(8,128)(2,1)} %get-tuple-element.89), channel_id=1, source_target_pairs={{0,1},{1,0},{2,3},{3,2},{4,5},{5,4},{6,7},{7,6},{8,9},{9,8},{10,11... | collective-permute-start | bytes 1474568 | tf_op jit(solution)/shard_map/ppermute | solution.py:640
  116.9 81.2 %collective-permute-start.26 = (bf16[24,1792]{1,0:T(8,128)(2,1)}, bf16[24,1792]{1,0:T(8,128)(2,1)S(1)}, u32[]{:S(2)}, u32[]{:S(2)}) collective-permute-start(bf16[24,1792]{1,0:T(8,128)(2,1)} %get-tuple-element.107), channel_id=1, source_target_pairs={{0,8},{1,9},{2,10},{3,11},{4,12},{5,13},{6,14},{7,15},{8,0},{9,1},... | collective-permute-start | bytes 258056 | tf_op jit(solution)/shard_map/ppermute | solution.py:640
  157.0 46.6 %collective-permute-start.27 = (bf16[24,1792]{1,0:T(8,128)(2,1)}, bf16[24,1792]{1,0:T(8,128)(2,1)S(1)}, u32[]{:S(2)}, u32[]{:S(2)}) collective-permute-start(bf16[24,1792]{1,0:T(8,128)(2,1)} %get-tuple-element.108), channel_id=1, source_target_pairs={{0,16},{1,17},{2,18},{3,19},{4,20},{5,21},{6,22},{7,23},{8,24},{9,... | collective-permute-start | bytes 258056 | tf_op jit(solution)/shard_map/ppermute | solution.py:640
  215.8 12.3 %collective-permute-start.12 = (bf16[96,640]{1,0:T(8,128)(2,1)}, bf16[96,640]{1,0:T(8,128)(2,1)S(1)}, u32[]{:S(2)}, u32[]{:S(2)}) collective-permute-start(bf16[96,640]{1,0:T(8,128)(2,1)} %get-tuple-element.91), channel_id=1, source_target_pairs={{0,4},{1,5},{2,6},{3,7},{4,0},{5,1},{6,2},{7,3},{8,12},{9,13},{10,... | collective-permute-start | bytes 368648 | tf_op jit(solution)/shard_map/ppermute | solution.py:640
  228.1 39.4 %collective-permute-start.32 = (bf16[96,1792]{1,0:T(8,128)(2,1)}, bf16[96,1792]{1,0:T(8,128)(2,1)S(1)}, u32[]{:S(2)}, u32[]{:S(2)}) collective-permute-start(bf16[96,1792]{1,0:T(8,128)(2,1)} %get-tuple-element.110.refs_1_), channel_id=1, source_target_pairs={{0,4},{1,5},{2,6},{3,7},{4,0},{5,1},{6,2},{7,3},{8,12},{9,13},{10,... | collective-permute-start | bytes 1032200 | tf_op jit(solution)/shard_map/ppermute | solution.py:640
  261.5 11.0 %collective-permute-start.33 = (bf16[96,640]{1,0:T(8,128)(2,1)}, bf16[96,640]{1,0:T(8,128)(2,1)S(1)}, u32[]{:S(2)}, u32[]{:S(2)}) collective-permute-start(bf16[96,640]{1,0:T(8,128)(2,1)} %get-tuple-element.117), channel_id=1, source_target_pairs={{0,2},{1,3},{2,0},{3,1},{4,6},{5,7},{6,4},{7,5},{8,10},{9,11},{10,... | collective-permute-start | bytes 368648 | tf_op jit(solution)/shard_map/ppermute | solution.py:640
  272.5 10.9 %collective-permute-start.39 = (bf16[96,1792]{1,0:T(8,128)(2,1)S(1)}, bf16[96,1792]{1,0:T(8,128)(2,1)}, u32[]{:S(2)}, u32[]{:S(2)}) collective-permute-start(bf16[96,1792]{1,0:T(8,128)(2,1)S(1)} %copy-done.31), channel_id=1, source_target_pairs={{0,6},{1,7},{2,4},{3,5},{4,2},{5,3},{6,0},{7,1},{8,14},{9,15},{10,... | collective-permute-start | bytes 1032200 | tf_op jit(solution)/shard_map/ppermute | solution.py:640
  273.9 16.8 %collective-permute-start.38 = (bf16[96,1792]{1,0:T(8,128)(2,1)S(1)}, bf16[96,1792]{1,0:T(8,128)(2,1)}, u32[]{:S(2)}, u32[]{:S(2)}) collective-permute-start(bf16[96,1792]{1,0:T(8,128)(2,1)S(1)} %copy-done.31), channel_id=1, source_target_pairs={{0,2},{1,3},{2,0},{3,1},{4,6},{5,7},{6,4},{7,5},{8,10},{9,11},{10,... | collective-permute-start | bytes 1032200 | tf_op jit(solution)/shard_map/ppermute | solution.py:640
  275.4 28.9 %collective-permute-start.40 = (bf16[2,96,1792]{2,1,0:T(8,128)(2,1)}, bf16[2,96,1792]{2,1,0:T(8,128)(2,1)S(1)}, u32[]{:S(2)}, u32[]{:S(2)}) collective-permute-start(bf16[2,96,1792]{2,1,0:T(8,128)(2,1)} %get-tuple-element.118.rest_6_.rest_0_), channel_id=1, source_target_pairs={{0,1},{1,0},{2,3},{3,2},{4,5},{5,4},{6,7},{7,6},{8,9},{9,8},{10,11... | collective-permute-start | bytes 2064392 | tf_op jit(solution)/shard_map/ppermute | solution.py:640
  283.4 20.8 %collective-permute-start.42 = (bf16[96,1792]{1,0:T(8,128)(2,1)}, bf16[96,1792]{1,0:T(8,128)(2,1)}, u32[]{:S(2)}, u32[]{:S(2)}) collective-permute-start(bf16[96,1792]{1,0:T(8,128)(2,1)} %collective-permute-done.39.rest_8_.rest_2_), channel_id=1, source_target_pairs={{0,1},{1,0},{2,3},{3,2},{4,5},{5,4},{6,7},{7,6},{8,9},{9,8},{10,11... | collective-permute-start | bytes 1032200 | tf_op jit(solution)/shard_map/ppermute | solution.py:640
  290.7 13.6 %collective-permute-start.41 = (bf16[96,1792]{1,0:T(8,128)(2,1)}, bf16[96,1792]{1,0:T(8,128)(2,1)S(1)}, u32[]{:S(2)}, u32[]{:S(2)}) collective-permute-start(bf16[96,1792]{1,0:T(8,128)(2,1)} %collective-permute-done.38.rest_7_.rest_1_), channel_id=1, source_target_pairs={{0,1},{1,0},{2,3},{3,2},{4,5},{5,4},{6,7},{7,6},{8,9},{9,8},{10,11... | collective-permute-start | bytes 1032200 | tf_op jit(solution)/shard_map/ppermute | solution.py:640
  319.2 14.7 %collective-permute-start.43 = (f32[96,1152]{1,0:T(8,128)}, f32[96,1152]{1,0:T(8,128)S(1)}, u32[]{:S(2)}, u32[]{:S(2)}) collective-permute-start(f32[96,1152]{1,0:T(8,128)} %get-tuple-element.121), channel_id=1, source_target_pairs={{0,1},{1,0},{2,3},{3,2},{4,5},{5,4},{6,7},{7,6},{8,9},{9,8},{10,11... | collective-permute-start | bytes 1327112 | tf_op jit(solution)/shard_map/ppermute | solution.py:640
  (59 other events, 354.6 us)

commit v2 on v1

--- a/solution.py
+++ b/solution.py
@@ -32,10 +32,7 @@
 EPS = 1e-6
 NV = 12
 Q_COLS = 3 * D + 128
-R_COLS = D + 2 * F
-F2 = F // 2
-M_HALF = 256 + F
-Q_HALF = Q_COLS // 2
+R_COLS = D + 2 * F + 128
 f32 = jnp.float32
 bf16 = jnp.bfloat16
 SCALE = 1.0 / math.sqrt(HD)
@@ -242,9 +239,8 @@
             o1, d1 = dot_nt(u, w[:, cols(D + F, j)]), dot_nt(dzb, w[:, cols(D, j)])
             out_s[...] = o1 if first else out_s[...] + o1
             dc_s[...] = d1 if first else dc_s[...] + d1
-            base = M_HALF * (j // (steps // 2)) + 256
-            acc[:, cols(base, j % (steps // 2))] += dot(ct_s[...], dzb)
-            acc[:, cols(base + F2, j % (steps // 2))] += dot(dyt_s[...], u)
+            acc[:, cols(D, j)] += dot(ct_s[...], dzb)
+            acc[:, cols(D + F, j)] += dot(dyt_s[...], u)
 
         produce(0, 0)
         produce(1, 1)
@@ -260,9 +256,7 @@
         dh = dyf + norm_back(dc * g2, n2, r2)
         dh_ref[0] = dh
         dhb = dh.astype(bf16)
-        ot = o.T
-        acc[:, :256] += dot(ot, dhb[:, :256])
-        acc[:, M_HALF : M_HALF + 128] += dot(ot, dhb[:, 256:])
+        acc[:, :D] += dot(o.T, dhb)
         do_ref[0] = dot_nt(dhb, w[:, :D]).astype(bf16)
         vg[0:8] += col8(dc * n2)
         vg[8:16] += col8(dh)
@@ -403,13 +397,13 @@
 
 def mlp(n, slots, x, c_own, c_got, o, vec, pieces):
     rows = c_own.shape[0]
-    r_shape, r_spec = reduced(len(pieces), 2 * M_HALF)
+    r_shape, r_spec = reduced(len(pieces), R_COLS)
     return layer_call(
         mlp_kernel, n, slots, (x, c_own, c_got, o, vec),
         (item(TP, D), once((rows, D)), once((rows, D)), item(TP, D), whole((16, D))), pieces,
         (S((rows, D), bf16), S((slots, TP, D), f32), S((slots, TP, D), bf16)) + r_shape + (S((8, D), f32),),
         (once((rows, D)), item(TP, D), item(TP, D)) + r_spec + (whole((8, D)),),
-        (pltpu.VMEM((D, R_COLS), bf16), pltpu.VMEM((D, 2 * M_HALF), f32), pltpu.VMEM((32, D), f32),
+        (pltpu.VMEM((D, R_COLS), bf16), pltpu.VMEM((D, R_COLS), f32), pltpu.VMEM((32, D), f32),
          pltpu.VMEM((8, F), f32), pltpu.VMEM((D // 128, TP * slots, 128), f32), pltpu.VMEM((D // 128, TP * slots, 128), f32),
          pltpu.VMEM((1, F), f32), pltpu.VMEM((TP, D), bf16), pltpu.VMEM((TP, D), bf16), pltpu.VMEM((D, TP), bf16),
          pltpu.VMEM((D, TP), bf16), pltpu.VMEM((3, TP, FC), f32), pltpu.VMEM((3, TP, FC), f32),
@@ -442,6 +436,7 @@
     o_ref[:, :D] = p_ref[...].astype(bf16)
     o_ref[:, D : D + F] = a_ref[...].astype(bf16)
     o_ref[:, D + F : D + 2 * F] = b_ref[...].astype(bf16)
+    o_ref[:, D + 2 * F :] = jnp.zeros((o_ref.shape[0], R_COLS - D - 2 * F), bf16)
 
 
 def split3(a):
@@ -451,6 +446,14 @@
 
 def dot3(a, b):
     return dot(jnp.concatenate([a[0], a[1], a[0]], axis=1), jnp.concatenate([b[0], b[0], b[1]], axis=0))
+
+
+def dot3_sym(a, b):
+    left = jnp.concatenate([a[0], a[1], a[0]], axis=1)
+    right = jnp.concatenate([b[0], b[0], b[1]], axis=0)
+    wide = dot(left, right[:, :256])
+    corner = dot(left[256:], right[:, 256:])
+    return jnp.concatenate([wide, jnp.concatenate([wide[256:].T, corner], axis=0)], axis=1)
 
 
 def orth_rows(m, q_s, at, rows):
@@ -463,7 +466,7 @@
     q = None
     for k in range(NS_ITERS - 1):
         a_s = split3(a)
-        p = eye + COEFF_SECOND * a + COEFF_THIRD * dot3(a_s, a_s)
+        p = eye + COEFF_SECOND * a + COEFF_THIRD * dot3_sym(a_s, a_s)
         p_s = split3(p)
         if k == 0:
             q_s[...] = p
@@ -471,7 +474,7 @@
         else:
             q = dot3(split3(q), p_s)
         if k < NS_ITERS - 2:
-            a = dot3(split3(dot3(p_s, a_s)), p_s)
+            a = dot3_sym(split3(dot3_sym(p_s, a_s)), p_s)
 
     def times_last(v):
         return dot3(split3(dot3(split3(dot3(split3(v), p_s)), a_s)), p_s)
@@ -482,25 +485,17 @@
     return dot(hi, m) + dot(lo, m)
 
 
-def fetch_momenta(n_ref, pieces, buf, sems, plan):
-    rows = pieces[0].shape[1]
-
-    def start(x):
-        copies = []
-        for k in range(2):
-            own, near, far = pieces[3 * k : 3 * k + 3]
-            for off, src, h in ((0, own.at[0], 0), (0, own.at[1], 1), (2, near, x), (2, far, 1 - x)):
-                col, width, to = plan(h)
-                at = pl.multiple_of((n_ref[0] ^ (k + off)) * rows, 32)
-                copies.append(pltpu.make_async_copy(
-                    src.at[:, pl.ds(col, width)], buf.at[pl.ds(at, rows), pl.ds(to, width)], sems.at[len(copies)]))
-        for c in copies:
-            c.start()
-        for c in copies:
-            c.wait()
-
-    for x in range(2):
-        pl.when(n_ref[1] == x)(lambda x=x: start(x))
+def fetch_cols(n_ref, pieces, buf, sems, at_col, cols):
+    rows = pieces[0].shape[0]
+    copies = []
+    for k, piece in enumerate(pieces):
+        at = pl.multiple_of((n_ref[0] ^ k) * rows, 32)
+        copies.append(pltpu.make_async_copy(
+            piece.at[:, pl.ds(at_col, cols)], buf.at[pl.ds(at, rows), pl.ds(0, cols)], sems.at[k]))
+    for c in copies:
+        c.start()
+    for c in copies:
+        c.wait()
 
 
 def orth_both(n_ref, mine_ref, theirs_ref, m, q_s, o_s):
@@ -512,163 +507,42 @@
     theirs_ref[...] = o_s[pl.ds(pl.multiple_of((1 - core) * rows, 32), rows), :]
 
 
-def orth_mlp_kernel(n_ref, *rest):
-    pieces = rest[:6]
-    mine_ref, theirs_ref, m, q_s, o_s, sems = rest[6:]
-    at = pl.multiple_of(256 + (n_ref[0] & 1) * F2, 128)
-    fetch_momenta(n_ref, pieces, m, sems, lambda h: (at, F2, h * F2))
+def orth_mlp_kernel(parts, n_ref, *rest):
+    pieces = rest[:parts]
+    mine_ref, theirs_ref, m, q_s, o_s, sems = rest[parts:]
+    fetch_cols(n_ref, pieces, m, sems, pl.multiple_of(D + (n_ref[0] & 1) * F, 128), F)
     orth_both(n_ref, mine_ref, theirs_ref, m, q_s, o_s)
 
 
-def orth_attn_kernel(n_ref, *rest):
-    pieces, others = rest[:6], rest[6:12]
-    mine_ref, theirs_ref, m, q_s, o_s, sems = rest[12:]
+def orth_attn_kernel(parts, n_ref, *rest):
+    pieces, others = rest[:parts], rest[parts : 2 * parts]
+    mine_ref, theirs_ref, m, q_s, o_s, sems = rest[2 * parts :]
 
     @pl.when(n_ref[0] & 1 == 0)
     def _():
-        fetch_momenta(n_ref, pieces, m, sems, lambda h: (0, 3 * D - Q_HALF if h else Q_HALF, h * Q_HALF))
+        fetch_cols(n_ref, pieces, m, sems, 0, 3 * D)
 
     @pl.when(n_ref[0] & 1 == 1)
     def _():
         m[:, D:] = jnp.zeros((D, 2 * D), bf16)
-        fetch_momenta(n_ref, others, m, sems, lambda h: (0, D - 256 if h else 256, h * 256))
+        fetch_cols(n_ref, others, m, sems, 0, D)
 
     orth_both(n_ref, mine_ref, theirs_ref, m, q_s, o_s)
 
 
-def orth_call(kernel, at, pieces, cols):
-    rows = pieces[0].shape[1]
+def orth_call(kernel, me, pieces, more, cols):
+    parts = len(pieces)
+    rows = pieces[0].shape[0]
     spec = pl.BlockSpec((rows, cols), lambda i, n: (0, 0))
     return pl.pallas_call(
-        kernel, out_shape=(S((rows, cols), f32),) * 2,
+        lambda *refs: kernel(parts, *refs),
+        out_shape=(S((rows, cols), f32),) * 2,
         grid_spec=pltpu.PrefetchScalarGridSpec(
-            num_scalar_prefetch=1, grid=(1,), in_specs=[ANY] * len(pieces), out_specs=(spec,) * 2,
+            num_scalar_prefetch=1, grid=(1,), in_specs=[ANY] * (parts + len(more)), out_specs=(spec,) * 2,
             scratch_shapes=[pltpu.VMEM((D, cols), bf16), pltpu.VMEM((D, D), f32), pltpu.VMEM((2 * rows, cols), f32),
-                            pltpu.SemaphoreType.DMA((8,))]),
+                            pltpu.SemaphoreType.DMA((parts,))]),
         compiler_params=pltpu.CompilerParams(vmem_limit_bytes=VMEM_LIMIT),
-        cost_estimate=pl.CostEstimate(flops=8_000_000_000, bytes_accessed=4_000_000, transcendentals=0))(at, *pieces)
-
-
-def step_call(kernel, at, ins, outs, scratch):
-    full = [pl.BlockSpec(v.shape, lambda i, n, r=len(v.shape): (0,) * r) for v in ins]
-    return pl.pallas_call(
-        kernel, out_shape=outs,
-        grid_spec=pltpu.PrefetchScalarGridSpec(
-            num_scalar_prefetch=1, grid=(1,), in_specs=full,
-            out_specs=tuple(pl.BlockSpec(v.shape, lambda i, n, r=len(v.shape): (0,) * r) for v in outs),
-            scratch_shapes=scratch),
-        compiler_params=pltpu.CompilerParams(vmem_limit_bytes=VMEM_LIMIT),
-        cost_estimate=pl.CostEstimate(flops=1_000_000, bytes_accessed=1_000_000, transcendentals=0))(at, *ins)
-
-
-def split_xy_kernel(n_ref, keep_ref, got_ref, own_ref, x_ref, y_ref, xy_ref):
-    half = own_ref.shape[1]
-
-    def term(dy, dx):
-        y, at = n_ref[0] >> 1 ^ dy, pl.multiple_of((n_ref[1] ^ dx) * half, 128)
-        return keep_ref[y, :, pl.ds(at, half)] + got_ref[y, :, pl.ds(at, half)].astype(f32)
-
-    own_ref[...] = term(0, 0)
-    x_ref[...] = term(0, 1).astype(bf16)
-    y_ref[...] = term(1, 0).astype(bf16)
-    xy_ref[...] = term(1, 1).astype(bf16)
-
-
-def split_z_kernel(n_ref, own_ref, a_ref, b_ref, c_ref, keep_ref, *rest):
-    sends, t = rest[:3], rest[3]
-    t[...] = own_ref[...] + (a_ref[...].astype(f32) + b_ref[...].astype(f32) + c_ref[...].astype(f32))
-    rows = keep_ref.shape[0]
-    keep_ref[...] = t[pl.ds(pl.multiple_of(n_ref[2] * rows, 8), rows), :]
-    for k, ref in enumerate(sends):
-        ref[...] = t[pl.ds(pl.multiple_of((n_ref[2] ^ (k + 1)) * rows, 8), rows), :].astype(bf16)
-
-
-def sum_z_kernel(n_ref, own_ref, a_ref, b_ref, c_ref, o_ref):
-    t = own_ref[...] + (a_ref[...].astype(f32) + b_ref[...].astype(f32) + c_ref[...].astype(f32))
-    o_ref[...] = t.astype(o_ref.dtype)
-
-
-def momentum(g, mom, scale):
-    return MUON_MOMENTUM * mom + g.astype(f32) * scale
-
-
-def momenta_kernel(scale, plan, n_ref, own_ref, a_ref, b_ref, c_ref, *rest):
-    moms, (g_ref, m_ref) = rest[:-2], rest[-2:]
-    rows = own_ref.shape[0]
-    for k, ref in enumerate((own_ref, a_ref, b_ref, c_ref)):
-        g_ref[pl.ds(pl.multiple_of((n_ref[2] ^ k) * rows, 8), rows), :] = ref[...]
-    m_ref[...] = jnp.zeros_like(m_ref)
-
-    def fill(h):
-        for which, col, width, at in plan(h):
-            m_ref[:, at : at + width] = momentum(
-                g_ref[:, at : at + width], moms[which][:, col : col + width], scale).astype(bf16)
-
-    for h in range(2):
-        pl.when(n_ref[1] == h)(lambda h=h: fill(h))
-
-
-def results_kernel(scale, plan, count, n_ref, own_ref, got_ref, *rest):
-    moms, grads, nexts, m_ref = rest[:count], rest[count : 2 * count], rest[2 * count : 3 * count], rest[3 * count]
-    m_ref[...] = jnp.zeros_like(m_ref)
-
-    def fill(x):
-        for h in range(2):
-            src = own_ref if h == x else got_ref
-            for which, col, width, at in plan(h):
-                g = src[:, at : at + width]
-                m = momentum(g, moms[which][:, col : col + width], scale)
-                grads[which][:, col : col + width] = g.astype(f32) * scale
-                nexts[which][:, col : col + width] = m
-                m_ref[h, :, at : at + width] = m.astype(bf16)
-
-    for x in range(2):
-        pl.when(n_ref[1] == x)(lambda x=x: fill(x))
-
-
-def mlp_plan(h):
-    return ((0, 256 * h, D - 256 if h else 256, 0), (1, F2 * h, F2, 256), (2, F2 * h, F2, 256 + F2))
-
-
-def attn_plan(h):
-    return ((0, Q_HALF * h, 3 * D - Q_HALF if h else Q_HALF, 0),)
-
-
-def send(v, rep, fsdp):
-    parts = lax.axis_size("fsdp")
-    pairs = [(r * parts + f, (r ^ rep) * parts + (f ^ fsdp)) for r in range(lax.axis_size("rep")) for f in range(parts)]
-    return lax.ppermute(v, ("rep", "fsdp"), pairs)
-
-
-def spread_xy(at, sent, keep):
-    got = send(sent, 0, 1)
-    half = S((keep.shape[1], keep.shape[2] // 2), bf16)
-    own, to_x, to_y, to_xy = step_call(
-        split_xy_kernel, at, (keep, got), (S(half.shape, f32), half, half, half), [])
-    return own, send(to_x, 1, 0), send(to_y, 0, 2), send(to_xy, 1, 2)
-
-
-def sum_all(at, terms, moms, plan, scale):
-    rows, half = terms[0].shape
-    z = S((rows // 4, half), bf16)
-    out = step_call(split_z_kernel, at, terms, (S(z.shape, f32), z, z, z), [pltpu.VMEM((rows, half), f32)])
-    got = [send(v, 2 * (k + 1), 0) for k, v in enumerate(out[1:])]
-    more = range(3, lax.axis_size("rep").bit_length() - 1)
-    (g,) = step_call(sum_z_kernel, at, (out[0], *got), (S(z.shape, f32 if more else bf16),), [])
-    for b in more:
-        g = g.astype(bf16).astype(f32) + send(g.astype(bf16), 1 << b, 0).astype(f32)
-    g = g.astype(bf16)
-    got = [send(g, 2 * k, 0) for k in range(1, 4)]
-    both = S((rows, half), bf16)
-    g, m = step_call(lambda *refs: momenta_kernel(scale, plan, *refs), at, (g, *got, *moms), (both, both), [])
-    near, far, g_x = send(m, 0, 2), send(m, 1, 2), send(g, 1, 0)
-    count = len(moms)
-    full = tuple(S(v.shape, f32) for v in moms)
-    out = step_call(lambda *refs: results_kernel(scale, plan, count, *refs), at, (g, g_x, *moms),
-                    full + full + (S((2, rows, half), bf16),), [])
-    own = out[-1]
-    pieces = [own, near, far] + [send(v, 0, 1) for v in (own, near, far)]
-    return g, g_x, out[:count], out[count : 2 * count], pieces
+        cost_estimate=pl.CostEstimate(flops=8_000_000_000, bytes_accessed=4_000_000, transcendentals=0))(me, *pieces, *more)
 
 
 def swap(v, axis, k):
@@ -677,6 +551,10 @@
 
 def bits(axis):
     return range(lax.axis_size(axis).bit_length() - 1)
+
+
+def bit(axis, b):
+    return (lax.axis_index(axis) >> b) & 1
 
 
 def all_pieces(v, axis):
@@ -684,6 +562,51 @@
     for b in reversed(bits(axis)):
         pieces.update({k ^ (1 << b): swap(p, axis, 1 << b) for k, p in list(pieces.items())})
     return [pieces[k] for k in range(lax.axis_size(axis))]
+
+
+def take(v, i):
+    return lax.dynamic_index_in_dim(v, i, 0, keepdims=False)
+
+
+def sum_blocks(send, keep):
+    got = swap(send, "fsdp", 1)
+    keep, got = (v.reshape((2, -1) + v.shape[1:]) for v in (keep, got))
+    for b in reversed(bits("fsdp")[1:]):
+        me = bit("fsdp", b)
+        sent = (take(keep, 1 - me) + take(got, 1 - me).astype(f32)).astype(bf16)
+        own = take(keep, me) + take(got, me).astype(f32)
+        got = swap(sent, "fsdp", 1 << b)
+        keep = own
+        if keep.shape[0] > 1:
+            keep, got = (v.reshape((2, -1) + v.shape[1:]) for v in (keep, got))
+    return (keep + got.astype(f32)).reshape(keep.shape[-2:])
+
+
+def halves(v, axis):
+    n = v.shape[axis] // 2
+    return lax.slice_in_dim(v, 0, n, axis=axis), lax.slice_in_dim(v, n, 2 * n, axis=axis)
+
+
+def sum_groups(v):
+    for b in bits("rep"):
+        me = bit("rep", b)
+        lo, hi = halves(v, 1 if b == 0 else 0)
+        got = swap(jnp.where(me == 0, hi, lo).astype(bf16), "rep", 1 << b)
+        v = jnp.where(me == 0, lo, hi) + got.astype(f32)
+    v = v.astype(bf16)
+    for b in reversed(bits("rep")):
+        me = bit("rep", b)
+        got = swap(v, "rep", 1 << b)
+        v = jnp.concatenate([jnp.where(me == 0, v, got), jnp.where(me == 0, got, v)], axis=1 if b == 0 else 0)
+    return v
+
+
+def sum_groups_whole(v):
+    v = v.astype(bf16)
+    for b in bits("rep"):
+        got = swap(v, "rep", 1 << b)
+        v = (v.astype(f32) + got.astype(f32)).astype(bf16)
+    return v
 
 
 def unpool_kernel(slots, n_ref, own_ref, got_ref, o_ref):
@@ -704,10 +627,9 @@
         cost_estimate=pl.CostEstimate(flops=1_000_000, bytes_accessed=7_000_000, transcendentals=0))(count, own, got)
 
 
-def adam_kernel(scale, n_ref, own_ref, got_ref, *refs):
+def adam_kernel(scale, g_ref, *refs):
     ins, outs = refs[:6], refs[6:]
-    g = jnp.where(n_ref[1] == 1, own_ref[...], got_ref[...])
-    g = (g.astype(f32) * scale).T
+    g = (g_ref[...].astype(f32) * scale).T
     for k, (lo, hi) in enumerate(((0, 2), (2, NV))):
         gradient, parameter = g[lo:hi], ins[k][...]
         first = ADAM_FIRST * ins[2 + 2 * k][...] + (1.0 - ADAM_FIRST) * gradient
@@ -721,16 +643,14 @@
         outs[5 + 2 * k][...] = second
 
 
-def adam(at, own, got, devices, *states):
-    full = [pl.BlockSpec(v.shape, lambda i, n: (0, 0)) for v in states]
+def adam(last, devices, *states):
+    full = [pl.BlockSpec(v.shape, lambda i: (0, 0)) for v in states]
     one, two = S(states[0].shape, f32), S(states[1].shape, f32)
-    last = pl.BlockSpec((own.shape[0], 128), lambda i, n: (0, Q_HALF // 128 - 1))
     return pl.pallas_call(
         lambda *refs: adam_kernel(1.0 / devices, *refs),
-        out_shape=(one, two, one, two, one, one, two, two),
-        grid_spec=pltpu.PrefetchScalarGridSpec(
-            num_scalar_prefetch=1, grid=(1,), in_specs=[last, last] + full,
-            out_specs=tuple(full[k] for k in (0, 1, 0, 1, 2, 3, 4, 5))), name="adam")(at, own, got, *states)
+        grid=(1,), out_shape=(one, two, one, two, one, one, two, two),
+        in_specs=[pl.BlockSpec((last.shape[0], 128), lambda i: (0, 3 * D // 128))] + full,
+        out_specs=tuple(full[k] for k in (0, 1, 0, 1, 2, 3, 4, 5)), name="adam")(last, *states)
 
 
 def muon_factor(row_total, column_total):
@@ -763,29 +683,33 @@
     rest = pl.pallas_call(pack_rest_kernel, out_shape=S((rows, R_COLS), bf16), name="pack_rest")(w_proj, w_fc1, w_fc2.T)
     r_pieces = all_pieces(rest, "fsdp")
 
-    rep_at = lax.axis_index("rep").astype(jnp.int32)
-    at = jnp.stack([me, rep_at & 1, (rep_at >> 1) & 3])
     x, qkv, o, lse, vec = attn_fwd(n, slots, x_own, x_got, q_pieces)
     out, dh, do, r_send, r_keep, vb = mlp(n, slots, x, c_own, c_got, o, vec, r_pieces)
-    terms = spread_xy(at, r_send, r_keep)
+    mid = sum_blocks(r_send, r_keep)
     in_grad, q_send, q_keep = attn_bwd(n, slots, x, qkv, lse, do, dh, vec, vb, q_pieces, x_own.shape[0])
-    scale = 1.0 / devices
-    _, _, mid_grads, mid_nexts, mid_pieces = sum_all(
-        at, terms, (mom_proj, mom_fc1, mom_fc2.T), mlp_plan, scale)
-    g, g_x, (grad_qkv,), (next_qkv,), qkv_pieces = sum_all(
-        at, spread_xy(at, q_send, q_keep), (mom_qkv,), attn_plan, scale)
+    mid = sum_groups(mid)
+    last = sum_groups_whole(sum_blocks(q_send, q_keep))
     block_out = unpool(out)
     input_grad = unpool(in_grad)
-    vectors = adam(at, g, g_x, devices, gains, biases, gains_first, gains_second, biases_first, biases_second)
-    grad_proj, grad_fc1, grad_fc2t = mid_grads
-    next_proj, next_fc1, next_fc2t = mid_nexts
+
+    vectors = adam(last, devices, gains, biases, gains_first, gains_second, biases_first, biases_second)
+    last = last.astype(f32) * (1.0 / devices)
+    grad_qkv = last[:, : 3 * D]
+    next_qkv = MUON_MOMENTUM * mom_qkv + grad_qkv
+    qkv_pieces = all_pieces(next_qkv.astype(bf16), "fsdp")
+    mid = mid.astype(f32) * (1.0 / devices)
+    mom_mid = jnp.concatenate([mom_proj, mom_fc1, mom_fc2.T], axis=1)
+    next_mid = MUON_MOMENTUM * mom_mid + mid[:, : D + 2 * F]
+    mid_pieces = all_pieces(next_mid.astype(bf16), "fsdp")
+    grad_proj, grad_fc1, grad_fc2t = mid[:, :D], mid[:, D : D + F], mid[:, D + F : D + 2 * F]
+    next_proj, next_fc1, next_fc2t = next_mid[:, :D], next_mid[:, D : D + F], next_mid[:, D + F :]
 
     core = me & 1
-    mine, theirs = orth_call(orth_mlp_kernel, at, mid_pieces, F)
-    got = send(theirs, 0, 1)
+    mine, theirs = orth_call(orth_mlp_kernel, me.reshape(1), mid_pieces, [], F)
+    got = swap(theirs, "fsdp", 1)
     orth_fc1, orth_fc2t = jnp.where(core == 0, mine, got), jnp.where(core == 0, got, mine)
-    mine, theirs = orth_call(orth_attn_kernel, at, qkv_pieces + mid_pieces, 3 * D)
-    got = send(theirs, 0, 1)
+    mine, theirs = orth_call(orth_attn_kernel, me.reshape(1), qkv_pieces, mid_pieces, 3 * D)
+    got = swap(theirs, "fsdp", 1)
     orth_qkv, orth_proj = jnp.where(core == 0, mine, got), jnp.where(core == 0, got, mine)[:, :D]
     new_qkv = w_qkv - MUON_RATE * muon_factor(D, 3 * D) * orth_qkv
     new_proj = w_proj - MUON_RATE * muon_factor(D, D) * orth_proj

time: 338 us -> 291 us (0.86)
  Pallas kernels: 121 us -> 89.1 us
  starting transfers between devices: 122 us -> 111 us
  waiting for transfers between devices: 79 us -> 72.6 us
  other arithmetic: 3.95 us -> 9.29 us
    ppermute x34 -> x0, starting transfers between devices: 118 us -> none  [send(): return lax.ppermute(v, ('rep', 'fsdp'), pairs)]
    ppermute x11 -> x32, starting transfers between devices: 4.91 us -> 111 us  [swap(): lax.ppermute(v, axis, [(i, i ^ k) for i in range(lax.axis_size(axis))])]
    ppermute x34 -> x0, waiting for transfers between devices: 60.4 us -> none  [send(): return lax.ppermute(v, ('rep', 'fsdp'), pairs)]
    ppermute x11 -> x32, waiting for transfers between devices: 18.7 us -> 72.6 us  [swap(): lax.ppermute(v, axis, [(i, i ^ k) for i in range(lax.axis_size(axis))])]
    pallas_call x13 -> x3, Pallas kernels: 59.5 us -> 27.9 us  [the longest x2 26.4 us: orth_call(): pl.pallas_call(lambda *refs: kernel(parts, *refs), out_shape=(S((rows, co...]
    unnamed x76 -> x36, local copies, waits for them, and re-layouts: 8.49 us -> 3.27 us
    convert_element_type x0 -> x12, other arithmetic: none -> 3.97 us  [the longest x2 1.5 us: sum_blocks(): sent = (take(keep, 1 - me) + take(got, 1 - me).astype(f32)).astype(bf16)]
  transfers between devices with their start and end apart: 45 -> 32, of which waited for: 17 -> 14; matrix products, arithmetic and copies ran while one was open for 1% -> 3% of each run, Pallas kernels for 25% -> 19%
where the time goes in v2:
time: 291 us; the launch traced here: 290 us
  starting transfers between devices  111 us (38%)
  Pallas kernels  89.1 us (31%)
  waiting for transfers between devices  72.6 us (25%)
  other arithmetic  9.29 us (3%)
  local copies, waits for them, and re-layouts  6.06 us (2%)
    ppermute x32, starting transfers between devices, swap(): lax.ppermute(v, axis, [(i, i ^ k) for i in range(lax.axis_size(axis))])  111 us
    ppermute x32, waiting for transfers between devices, swap(): lax.ppermute(v, axis, [(i, i ^ k) for i in range(lax.axis_size(axis))])  72.6 us
    pallas_call x3, Pallas kernels, layer_call(): pl.pallas_call(lambda *refs: kernel(parts, *refs), out_shape=outs, grid_s...  49.3 us
    pallas_call x2, Pallas kernels, orth_call(): pl.pallas_call(lambda *refs: kernel(parts, *refs), out_shape=(S((rows, co...  26.4 us
    pallas_call x2, Pallas kernels, unpool_call(): pl.pallas_call(lambda *refs: unpool_kernel(slots, *refs), out_shape=S(own...  7.86 us
  transfers between devices with their start and end apart: 32, of which 14 were waited for; matrix products, arithmetic and copies ran while one was open for 3% of the time, Pallas kernels for 19%

profile of v2, /device:TPU:0, one launch (start us, length us, event | category | flops | bytes accessed | tf_op | source)
XLA Modules:
  0.0 290.3 jit_solution(5259275673724093877)
XLA Ops:
  3.5 2.9 %collective-permute-start.7 = (bf16[96,3584]{1,0:T(8,128)(2,1)}, bf16[96,3584]{1,0:T(8,128)(2,1)S(1)}, u32[]{:S(2)}, u32[]{:S(2)}) collective-permute-start(bf16[96,3584]{1,0:T(8,128)(2,1)} %pack_rest.1.refs_6_), channel_id=1, source_target_pairs={{0,2},{1,3},{2,0},{3,1},{4,6},{5,7},{6,4},{7,5},{8,10},{9,11},{10,... | collective-permute-start | bytes 2064392 | tf_op jit(solution)/shard_map/ppermute | solution.py:549
  9.7 17.9 %collective-permute-done.3.refs_5_.refs_10_ = bf16[96,1280]{1,0:T(8,128)(2,1)S(1)} collective-permute-done((bf16[96,1280]{1,0:T(8,128)(2,1)}, bf16[96,1280]{1,0:T(8,128)(2,1)S(1)}, u32[]{:S(2)}, u32[]{:S(2)}) %collective-permute-start.3) | collective-permute-done | bytes 245792 | tf_op jit(solution)/shard_map/ppermute | solution.py:549
  30.1 12.1 %shard_map.336 = (bf16[16,208,384]{2,1,0:T(8,128)(2,1)}, bf16[16,208,1152]{2,1,0:T(8,128)(2,1)}, bf16[16,208,384]{2,1,0:T(8,128)(2,1)}, f32[16,208,128]{2,1,0:T(8,128)}, f32[16,384]{1,0:T(8,128)}) custom-call(s32[3]{0:T(128)} %pad_add_fusion.refs_0_, bf16[3152,384]{1,0:T(8,128)(2,1)} %bitcast.31, bf16[3152,384]{1,0:T(8,128)(2,1)} %collective-permute-done.1.refs_2_, ...), custom_call_target="tpu_custom_call" | custom-call | flops 10000000000 | bytes 20000000 | tf_op jit(solution)/shard_map/pallas_call | solution.py:368
  43.7 21.9 %shard_map.337 = (bf16[3152,384]{1,0:T(8,128)(2,1)}, f32[16,208,384]{2,1,0:T(8,128)}, bf16[16,208,384]{2,1,0:T(8,128)(2,1)}, bf16[2,96,3584]{2,1,0:T(8,128)(2,1)...) custom-call(s32[3]{0:T(128)} %pad_add_fusion.refs_0_, bf16[16,208,384]{2,1,0:T(8,128)(2,1)} %get-tuple-element.48.refs_1_, ...), custom_call_target="tpu_custom_call" | custom-call | flops 24999999488 | bytes 20000000 | tf_op jit(solution)/shard_map/pallas_call | solution.py:368
  66.1 3.0 %collective-permute-done.16 = bf16[2,96,3584]{2,1,0:T(8,128)(2,1)S(1)} collective-permute-done((bf16[2,96,3584]{2,1,0:T(8,128)(2,1)}, bf16[2,96,3584]{2,1,0:T(8,128)(2,1)S(1)}, u32[]{:S(2)}, u32[]{:S(2)}) %collective-permute-start.16) | collective-permute-done | bytes 1376288 | tf_op jit(solution)/shard_map/ppermute | solution.py:549
  70.5 6.8 %collective-permute-start.17 = (bf16[1,96,3584]{2,1,0:T(8,128)(2,1)S(1)}, bf16[1,96,3584]{2,1,0:T(8,128)(2,1)S(1)}, u32[]{:S(2)}, u32[]{:S(2)}) collective-permute-start(bf16[1,96,3584]{2,1,0:T(8,128)(2,1)S(1)} %add_convert_fusion), channel_id=1, source_target_pairs={{0,2},{1,3},{2,0},{3,1},{4,6},{5,7},{6,4},{7,5},{8,10},{9,11},{10,... | collective-permute-start | bytes 2064392 | tf_op jit(solution)/shard_map/ppermute | solution.py:549
  77.4 16.0 %collective-permute-done.17 = bf16[1,96,3584]{2,1,0:T(8,128)(2,1)S(1)} collective-permute-done((bf16[1,96,3584]{2,1,0:T(8,128)(2,1)S(1)}, bf16[1,96,3584]{2,1,0:T(8,128)(2,1)S(1)}, u32[]{:S(2)}, u32[]{:S(2)}) %collective-permute-start.17) | collective-permute-done | bytes 688160 | tf_op jit(solution)/shard_map/ppermute | solution.py:549
  96.2 8.6 %collective-permute-done.18 = bf16[96,1792]{1,0:T(8,128)(2,1)S(1)} collective-permute-done((bf16[96,1792]{1,0:T(8,128)(2,1)S(1)}, bf16[96,1792]{1,0:T(8,128)(2,1)S(1)}, u32[]{:S(2)}, u32[]{:S(2)}) %collective-permute-start.18) | collective-permute-done | bytes 344096 | tf_op jit(solution)/shard_map/ppermute | solution.py:549
  104.9 26.7 %collective-permute-start.19 = (bf16[48,1792]{1,0:T(8,128)(2,1)S(1)}, bf16[48,1792]{1,0:T(8,128)(2,1)S(1)}, u32[]{:S(2)}, u32[]{:S(2)}) collective-permute-start(bf16[48,1792]{1,0:T(8,128)(2,1)S(1)} %select_convert_fusion.1), channel_id=1, source_target_pairs={{0,8},{4,12},{8,0},{12,4},{16,24},{20,28},{24,16},{28,20},{1,9},{5... | collective-permute-start | bytes 516104 | tf_op jit(solution)/shard_map/ppermute | solution.py:549
  131.7 15.3 %shard_map.339 = (bf16[3152,384]{1,0:T(8,128)(2,1)}, bf16[2,96,1280]{2,1,0:T(8,128)(2,1)}, f32[2,96,1280]{2,1,0:T(8,128)}) custom-call(s32[3]{0:T(128)} %pad_add_fusion.refs_0_, bf16[16,208,384]{2,1,0:T(8,128)(2,1)} %get-tuple-element.48.refs_1_, bf16[16,208,1152]{2,1,0:T(8,128)(2,1)} %get-tuple-element.52.refs_2_, ...), custom_call_target="tpu_custom_call" | custom-call | flops 20000000000 | bytes 20000000 | tf_op jit(solution)/shard_map/pallas_call | solution.py:368
  147.7 48.9 %collective-permute-start.20 = (bf16[24,1792]{1,0:T(8,128)(2,1)S(1)}, bf16[24,1792]{1,0:T(8,128)(2,1)S(1)}, u32[]{:S(2)}, u32[]{:S(2)}) collective-permute-start(bf16[24,1792]{1,0:T(8,128)(2,1)S(1)} %select_convert_fusion.2), channel_id=1, source_target_pairs={{0,16},{4,20},{8,24},{12,28},{16,0},{20,4},{24,8},{28,12},{1,17},{... | collective-permute-start | bytes 258056 | tf_op jit(solution)/shard_map/ppermute | solution.py:549
  196.8 3.0 %collective-permute-done.20 = bf16[24,1792]{1,0:T(8,128)(2,1)S(1)} collective-permute-done((bf16[24,1792]{1,0:T(8,128)(2,1)S(1)}, bf16[24,1792]{1,0:T(8,128)(2,1)S(1)}, u32[]{:S(2)}, u32[]{:S(2)}) %collective-permute-start.20) | collective-permute-done | bytes 86048 | tf_op jit(solution)/shard_map/ppermute | solution.py:549
  199.8 2.7 collective-permute-start.21
  204.9 4.2 %collective-permute-start.13 = (bf16[96,1280]{1,0:T(8,128)(2,1)S(1)}, bf16[96,1280]{1,0:T(8,128)(2,1)S(1)}, u32[]{:S(2)}, u32[]{:S(2)}) collective-permute-start(bf16[96,1280]{1,0:T(8,128)(2,1)S(1)} %fusion), channel_id=1, source_target_pairs={{0,4},{4,0},{8,12},{12,8},{16,20},{20,16},{24,28},{28,24},{1,5},{5... | collective-permute-start | bytes 737288 | tf_op jit(solution)/shard_map/ppermute | solution.py:549
  209.1 3.7 %collective-permute-start.22 = (bf16[48,1792]{1,0:T(8,128)(2,1)S(1)}, bf16[48,1792]{1,0:T(8,128)(2,1)S(1)}, u32[]{:S(2)}, u32[]{:S(2)}) collective-permute-start(bf16[48,1792]{1,0:T(8,128)(2,1)S(1)} %pad_maximum_fusion.1), channel_id=1, source_target_pairs={{0,8},{4,12},{8,0},{12,4},{16,24},{20,28},{24,16},{28,20},{1,9},{5... | collective-permute-start | bytes 516104 | tf_op jit(solution)/shard_map/ppermute | solution.py:549
  214.8 3.3 %collective-permute-start.14 = (bf16[96,1280]{1,0:T(8,128)(2,1)S(1)}, bf16[96,1280]{1,0:T(8,128)(2,1)S(1)}, u32[]{:S(2)}, u32[]{:S(2)}) collective-permute-start(bf16[96,1280]{1,0:T(8,128)(2,1)S(1)} %add_convert_fusion.3), channel_id=1, source_target_pairs={{0,8},{4,12},{8,0},{12,4},{16,24},{20,28},{24,16},{28,20},{1,9},{5... | collective-permute-start | bytes 737288 | tf_op jit(solution)/shard_map/ppermute | solution.py:549
  220.0 2.9 collective-permute-done.14
  222.9 2.8 collective-permute-start.15
  230.2 5.6 %collective-permute-done.15 = bf16[96,1280]{1,0:T(8,128)(2,1)S(1)} collective-permute-done((bf16[96,1280]{1,0:T(8,128)(2,1)S(1)}, bf16[96,1280]{1,0:T(8,128)(2,1)S(1)}, u32[]{:S(2)}, u32[]{:S(2)}) %collective-permute-start.15) | collective-permute-done | bytes 245792 | tf_op jit(solution)/shard_map/ppermute | solution.py:549
  237.8 8.3 %collective-permute-done.28.refs_7_.refs_3_ = bf16[96,3456]{1,0:T(8,128)(2,1)} collective-permute-done((bf16[96,3456]{1,0:T(8,128)(2,1)}, bf16[96,3456]{1,0:T(8,128)(2,1)}, u32[]{:S(2)}, u32[]{:S(2)}) %collective-permute-start.28) | collective-permute-done | bytes 663584 | tf_op jit(solution)/shard_map/ppermute | solution.py:549
  248.9 3.9 %shard_map.340 = bf16[3152,384]{1,0:T(8,128)(2,1)} custom-call(s32[1]{0:T(128)S(6)} %copy.39.refs_0_, bf16[3152,384]{1,0:T(8,128)(2,1)} %get-tuple-element.57.refs_1_, bf16[3152,384]{1,0:T(8,128)(2,1)} %collective-permute-done.10.refs_2_), custom_call_target="tpu_custom_call" | custom-call | flops 1000000 | bytes 7000000 | tf_op jit(solution)/shard_map/pallas_call | solution.py:623
  252.8 3.9 %shard_map.338 = bf16[3152,384]{1,0:T(8,128)(2,1)} custom-call(s32[1]{0:T(128)S(6)} %copy.39.refs_0_, bf16[3152,384]{1,0:T(8,128)(2,1)} %get-tuple-element.51.refs_1_, bf16[3152,384]{1,0:T(8,128)(2,1)} %collective-permute-done.9.refs_2_), custom_call_target="tpu_custom_call" | custom-call | flops 1000000 | bytes 7000000 | tf_op jit(solution)/shard_map/pallas_call | solution.py:623
  260.2 12.9 %shard_map.341 = (f32[96,1152]{1,0:T(8,128)}, f32[96,1152]{1,0:T(8,128)}) custom-call(s32[1]{0:T(128)} %bitcast.refs_0_, bf16[96,1152]{1,0:T(8,128)(2,1)} %copy-done.11, bf16[96,1152]{1,0:T(8,128)(2,1)} %copy-done.17, bf16[96,1152]{1,0:T(8,128)(2,1)} %copy-done.16, bf16[96,1152]{1,0:T(8,128)(2,1)} %collective-permute-done.26.refs_4_, ...), custom_call_target="tpu_custom_call" | custom-call | flops 8000000000 | bytes 4000000 | tf_op jit(solution)/shard_map/pallas_call | solution.py:537
  273.3 13.5 %shard_map.342 = (f32[96,1536]{1,0:T(8,128)}, f32[96,1536]{1,0:T(8,128)}) custom-call(s32[1]{0:T(128)} %bitcast.refs_0_, bf16[96,3456]{1,0:T(8,128)(2,1)} %get-tuple-element.74.refs_5_.refs_1_, bf16[96,3456]{1,0:T(8,128)(2,1)} %collective-permute-done.27.refs_6_.refs_2_, bf16[96,3456]{1,0:T(8,128)(2,1)} %collective-permute-done.28.refs_7_.refs_3_, ...), custom_call_target="tpu_custom_call" | custom-call | flops 8000000000 | bytes 4000000 | tf_op jit(solution)/shard_map/pallas_call | solution.py:537
  (114 shorter events, 37.2 us)
Async XLA Ops:
  0.7 29.5 %collective-permute-start.1 = (bf16[3152,384]{1,0:T(8,128)(2,1)}, bf16[3152,384]{1,0:T(8,128)(2,1)}, u32[]{:S(2)}, u32[]{:S(2)}) collective-permute-start(bf16[3152,384]{1,0:T(8,128)(2,1)} %bitcast.30), channel_id=1, source_target_pairs={{0,1},{1,0},{2,3},{3,2},{4,5},{5,4},{6,7},{7,6},{8,9},{9,8},{10,11... | collective-permute-start | bytes 7262216 | tf_op jit(solution)/shard_map/ppermute | solution.py:549
  1.2 41.1 %collective-permute-start.5 = (bf16[3152,384]{1,0:T(8,128)(2,1)}, bf16[3152,384]{1,0:T(8,128)(2,1)S(1)}, u32[]{:S(2)}, u32[]{:S(2)}) collective-permute-start(bf16[3152,384]{1,0:T(8,128)(2,1)} %bitcast.32), channel_id=1, source_target_pairs={{0,1},{1,0},{2,3},{3,2},{4,5},{5,4},{6,7},{7,6},{8,9},{9,8},{10,11... | collective-permute-start | bytes 7262216 | tf_op jit(solution)/shard_map/ppermute | solution.py:549
  3.5 26.5 %collective-permute-start.7 = (bf16[96,3584]{1,0:T(8,128)(2,1)}, bf16[96,3584]{1,0:T(8,128)(2,1)S(1)}, u32[]{:S(2)}, u32[]{:S(2)}) collective-permute-start(bf16[96,3584]{1,0:T(8,128)(2,1)} %pack_rest.1.refs_6_), channel_id=1, source_target_pairs={{0,2},{1,3},{2,0},{3,1},{4,6},{5,7},{6,4},{7,5},{8,10},{9,11},{10,... | collective-permute-start | bytes 2064392 | tf_op jit(solution)/shard_map/ppermute | solution.py:549
  8.2 19.3 %collective-permute-start.3 = (bf16[96,1280]{1,0:T(8,128)(2,1)}, bf16[96,1280]{1,0:T(8,128)(2,1)S(1)}, u32[]{:S(2)}, u32[]{:S(2)}) collective-permute-start(bf16[96,1280]{1,0:T(8,128)(2,1)} %pack_first.1.refs_3_.refs_8_), channel_id=1, source_target_pairs={{0,2},{1,3},{2,0},{3,1},{4,6},{5,7},{6,4},{7,5},{8,10},{9,11},{10,... | collective-permute-start | bytes 737288 | tf_op jit(solution)/shard_map/ppermute | solution.py:549
  9.5 20.0 %collective-permute-start.2 = (bf16[96,1280]{1,0:T(8,128)(2,1)}, bf16[96,1280]{1,0:T(8,128)(2,1)}, u32[]{:S(2)}, u32[]{:S(2)}) collective-permute-start(bf16[96,1280]{1,0:T(8,128)(2,1)} %pack_first.1.refs_3_.refs_8_), channel_id=1, source_target_pairs={{0,1},{1,0},{2,3},{3,2},{4,5},{5,4},{6,7},{7,6},{8,9},{9,8},{10,11... | collective-permute-start | bytes 737288 | tf_op jit(solution)/shard_map/ppermute | solution.py:549
  29.5 12.8 %collective-permute-start.6 = (bf16[96,3584]{1,0:T(8,128)(2,1)}, bf16[96,3584]{1,0:T(8,128)(2,1)}, u32[]{:S(2)}, u32[]{:S(2)}) collective-permute-start(bf16[96,3584]{1,0:T(8,128)(2,1)} %pack_rest.1.refs_6_), channel_id=1, source_target_pairs={{0,1},{1,0},{2,3},{3,2},{4,5},{5,4},{6,7},{7,6},{8,9},{9,8},{10,11... | collective-permute-start | bytes 2064392 | tf_op jit(solution)/shard_map/ppermute | solution.py:549
  30.0 12.2 %collective-permute-start.8 = (bf16[96,3584]{1,0:T(8,128)(2,1)S(1)}, bf16[96,3584]{1,0:T(8,128)(2,1)}, u32[]{:S(2)}, u32[]{:S(2)}) collective-permute-start(bf16[96,3584]{1,0:T(8,128)(2,1)S(1)} %collective-permute-done.7.refs_8_), channel_id=1, source_target_pairs={{0,1},{1,0},{2,3},{3,2},{4,5},{5,4},{6,7},{7,6},{8,9},{9,8},{10,11... | collective-permute-start | bytes 2064392 | tf_op jit(solution)/shard_map/ppermute | solution.py:549
  70.5 22.8 %collective-permute-start.17 = (bf16[1,96,3584]{2,1,0:T(8,128)(2,1)S(1)}, bf16[1,96,3584]{2,1,0:T(8,128)(2,1)S(1)}, u32[]{:S(2)}, u32[]{:S(2)}) collective-permute-start(bf16[1,96,3584]{2,1,0:T(8,128)(2,1)S(1)} %add_convert_fusion), channel_id=1, source_target_pairs={{0,2},{1,3},{2,0},{3,1},{4,6},{5,7},{6,4},{7,5},{8,10},{9,11},{10,... | collective-permute-start | bytes 2064392 | tf_op jit(solution)/shard_map/ppermute | solution.py:549
  94.9 9.8 %collective-permute-start.18 = (bf16[96,1792]{1,0:T(8,128)(2,1)S(1)}, bf16[96,1792]{1,0:T(8,128)(2,1)S(1)}, u32[]{:S(2)}, u32[]{:S(2)}) collective-permute-start(bf16[96,1792]{1,0:T(8,128)(2,1)S(1)} %select_convert_fusion), channel_id=1, source_target_pairs={{0,4},{4,0},{8,12},{12,8},{16,20},{20,16},{24,28},{28,24},{1,5},{5... | collective-permute-start | bytes 1032200 | tf_op jit(solution)/shard_map/ppermute | solution.py:549
  104.9 42.8 %collective-permute-start.19 = (bf16[48,1792]{1,0:T(8,128)(2,1)S(1)}, bf16[48,1792]{1,0:T(8,128)(2,1)S(1)}, u32[]{:S(2)}, u32[]{:S(2)}) collective-permute-start(bf16[48,1792]{1,0:T(8,128)(2,1)S(1)} %select_convert_fusion.1), channel_id=1, source_target_pairs={{0,8},{4,12},{8,0},{12,4},{16,24},{20,28},{24,16},{28,20},{1,9},{5... | collective-permute-start | bytes 516104 | tf_op jit(solution)/shard_map/ppermute | solution.py:549
  147.0 49.6 %collective-permute-start.11 = (bf16[2,96,1280]{2,1,0:T(8,128)(2,1)}, bf16[2,96,1280]{2,1,0:T(8,128)(2,1)S(1)}, u32[]{:S(2)}, u32[]{:S(2)}) collective-permute-start(bf16[2,96,1280]{2,1,0:T(8,128)(2,1)} %get-tuple-element.59), channel_id=1, source_target_pairs={{0,1},{1,0},{2,3},{3,2},{4,5},{5,4},{6,7},{7,6},{8,9},{9,8},{10,11... | collective-permute-start | bytes 1474568 | tf_op jit(solution)/shard_map/ppermute | solution.py:549
  147.1 101.3 %collective-permute-start.10 = (bf16[3152,384]{1,0:T(8,128)(2,1)}, bf16[3152,384]{1,0:T(8,128)(2,1)}, u32[]{:S(2)}, u32[]{:S(2)}) collective-permute-start(bf16[3152,384]{1,0:T(8,128)(2,1)} %get-tuple-element.57.refs_1_), channel_id=1, source_target_pairs={{0,1},{1,0},{2,3},{3,2},{4,5},{5,4},{6,7},{7,6},{8,9},{9,8},{10,11... | collective-permute-start | bytes 7262216 | tf_op jit(solution)/shard_map/ppermute | solution.py:549
  147.6 105.2 %collective-permute-start.9 = (bf16[3152,384]{1,0:T(8,128)(2,1)}, bf16[3152,384]{1,0:T(8,128)(2,1)}, u32[]{:S(2)}, u32[]{:S(2)}) collective-permute-start(bf16[3152,384]{1,0:T(8,128)(2,1)} %get-tuple-element.51.refs_1_), channel_id=1, source_target_pairs={{0,1},{1,0},{2,3},{3,2},{4,5},{5,4},{6,7},{7,6},{8,9},{9,8},{10,11... | collective-permute-start | bytes 7262216 | tf_op jit(solution)/shard_map/ppermute | solution.py:549
  147.7 52.0 %collective-permute-start.20 = (bf16[24,1792]{1,0:T(8,128)(2,1)S(1)}, bf16[24,1792]{1,0:T(8,128)(2,1)S(1)}, u32[]{:S(2)}, u32[]{:S(2)}) collective-permute-start(bf16[24,1792]{1,0:T(8,128)(2,1)S(1)} %select_convert_fusion.2), channel_id=1, source_target_pairs={{0,16},{4,20},{8,24},{12,28},{16,0},{20,4},{24,8},{28,12},{1,17},{... | collective-permute-start | bytes 258056 | tf_op jit(solution)/shard_map/ppermute | solution.py:549
  199.8 9.3 %collective-permute-start.21 = (bf16[24,1792]{1,0:T(8,128)(2,1)S(1)}, bf16[24,1792]{1,0:T(8,128)(2,1)S(1)}, u32[]{:S(2)}, u32[]{:S(2)}) collective-permute-start(bf16[24,1792]{1,0:T(8,128)(2,1)S(1)} %add_convert_fusion.6), channel_id=1, source_target_pairs={{0,16},{4,20},{8,24},{12,28},{16,0},{20,4},{24,8},{28,12},{1,17},{... | collective-permute-start | bytes 258056 | tf_op jit(solution)/shard_map/ppermute | solution.py:549
  204.9 9.9 %collective-permute-start.13 = (bf16[96,1280]{1,0:T(8,128)(2,1)S(1)}, bf16[96,1280]{1,0:T(8,128)(2,1)S(1)}, u32[]{:S(2)}, u32[]{:S(2)}) collective-permute-start(bf16[96,1280]{1,0:T(8,128)(2,1)S(1)} %fusion), channel_id=1, source_target_pairs={{0,4},{4,0},{8,12},{12,8},{16,20},{20,16},{24,28},{28,24},{1,5},{5... | collective-permute-start | bytes 737288 | tf_op jit(solution)/shard_map/ppermute | solution.py:549
  222.9 12.9 %collective-permute-start.15 = (bf16[96,1280]{1,0:T(8,128)(2,1)S(1)}, bf16[96,1280]{1,0:T(8,128)(2,1)S(1)}, u32[]{:S(2)}, u32[]{:S(2)}) collective-permute-start(bf16[96,1280]{1,0:T(8,128)(2,1)S(1)} %add_convert_fusion.2), channel_id=1, source_target_pairs={{0,16},{4,20},{8,24},{12,28},{16,0},{20,4},{24,8},{28,12},{1,17},{... | collective-permute-start | bytes 737288 | tf_op jit(solution)/shard_map/ppermute | solution.py:549
  229.1 17.0 %collective-permute-start.28 = (bf16[96,3456]{1,0:T(8,128)(2,1)}, bf16[96,3456]{1,0:T(8,128)(2,1)}, u32[]{:S(2)}, u32[]{:S(2)}) collective-permute-start(bf16[96,3456]{1,0:T(8,128)(2,1)} %get-tuple-element.74.refs_5_.refs_1_), channel_id=1, source_target_pairs={{0,2},{1,3},{2,0},{3,1},{4,6},{5,7},{6,4},{7,5},{8,10},{9,11},{10,... | collective-permute-start | bytes 1990664 | tf_op jit(solution)/shard_map/ppermute | solution.py:549
  236.9 11.4 %collective-permute-start.25 = (bf16[96,1152]{1,0:T(8,128)(2,1)S(1)}, bf16[96,1152]{1,0:T(8,128)(2,1)S(1)}, u32[]{:S(2)}, u32[]{:S(2)}) collective-permute-start(bf16[96,1152]{1,0:T(8,128)(2,1)S(1)} %get-tuple-element.76.refs_1_), channel_id=1, source_target_pairs={{0,2},{1,3},{2,0},{3,1},{4,6},{5,7},{6,4},{7,5},{8,10},{9,11},{10,... | collective-permute-start | bytes 663560 | tf_op jit(solution)/shard_map/ppermute | solution.py:549
  237.8 21.7 %collective-permute-start.27 = (bf16[96,3456]{1,0:T(8,128)(2,1)}, bf16[96,3456]{1,0:T(8,128)(2,1)}, u32[]{:S(2)}, u32[]{:S(2)}) collective-permute-start(bf16[96,3456]{1,0:T(8,128)(2,1)} %get-tuple-element.74.refs_5_.refs_1_), channel_id=1, source_target_pairs={{0,1},{1,0},{2,3},{3,2},{4,5},{5,4},{6,7},{7,6},{8,9},{9,8},{10,11... | collective-permute-start | bytes 1990664 | tf_op jit(solution)/shard_map/ppermute | solution.py:549
  246.1 13.5 %collective-permute-start.29 = (bf16[96,3456]{1,0:T(8,128)(2,1)}, bf16[96,3456]{1,0:T(8,128)(2,1)}, u32[]{:S(2)}, u32[]{:S(2)}) collective-permute-start(bf16[96,3456]{1,0:T(8,128)(2,1)} %collective-permute-done.28.refs_7_.refs_3_), channel_id=1, source_target_pairs={{0,1},{1,0},{2,3},{3,2},{4,5},{5,4},{6,7},{7,6},{8,9},{9,8},{10,11... | collective-permute-start | bytes 1990664 | tf_op jit(solution)/shard_map/ppermute | solution.py:549
  248.4 11.2 %collective-permute-start.24 = (bf16[96,1152]{1,0:T(8,128)(2,1)S(1)}, bf16[96,1152]{1,0:T(8,128)(2,1)S(1)}, u32[]{:S(2)}, u32[]{:S(2)}) collective-permute-start(bf16[96,1152]{1,0:T(8,128)(2,1)S(1)} %get-tuple-element.76.refs_1_), channel_id=1, source_target_pairs={{0,1},{1,0},{2,3},{3,2},{4,5},{5,4},{6,7},{7,6},{8,9},{9,8},{10,11... | collective-permute-start | bytes 663560 | tf_op jit(solution)/shard_map/ppermute | solution.py:549
  248.4 11.2 %collective-permute-start.26 = (bf16[96,1152]{1,0:T(8,128)(2,1)S(1)}, bf16[96,1152]{1,0:T(8,128)(2,1)}, u32[]{:S(2)}, u32[]{:S(2)}) collective-permute-start(bf16[96,1152]{1,0:T(8,128)(2,1)S(1)} %collective-permute-done.25.refs_3_), channel_id=1, source_target_pairs={{0,1},{1,0},{2,3},{3,2},{4,5},{5,4},{6,7},{7,6},{8,9},{9,8},{10,11... | collective-permute-start | bytes 663560 | tf_op jit(solution)/shard_map/ppermute | solution.py:549
  273.2 14.1 %collective-permute-start.30 = (f32[96,1152]{1,0:T(8,128)}, f32[96,1152]{1,0:T(8,128)S(1)}, u32[]{:S(2)}, u32[]{:S(2)}) collective-permute-start(f32[96,1152]{1,0:T(8,128)} %get-tuple-element.65), channel_id=1, source_target_pairs={{0,1},{1,0},{2,3},{3,2},{4,5},{5,4},{6,7},{7,6},{8,9},{9,8},{10,11... | collective-permute-start | bytes 1327112 | tf_op jit(solution)/shard_map/ppermute | solution.py:549
  (26 other events, 201.6 us)
